TPU v7x, 256 devices: a whole 4x4x8 slice. The times are simulated.
256 devices in a mesh: aux: 32 (over z, x), occ: 8 (over y, core).
Axes of the slice: x: 4, y: 4, z: 8, core: 2. Of those that a mesh axis runs over, the one named last changes fastest.
Arguments:
- half_integrals: float32 [2048, 256, 768], P('aux', 'occ'), may hold values from -2 to 2
- virtual_orbitals: float32 [768, 512], replicated, may hold values from -0.21875 to 0.21875
- occupied_energy: float32 [256], replicated, may hold values from -2 to -0.3
- virtual_energy: float32 [512], replicated, may hold values from 0.3 to 3
- partners: int32 [256, 1], replicated, may hold values from 0 to 255, as said below
Outputs:
- density: float32 [2048, 256, 512], P('aux', 'occ')
Inputs may be any that keep to these rules, and one draw needn't show every extreme that they name: `partners`: occupied orbitals form 8 groups of 32 consecutive ones; of the 32 entries of one group, at most 6 lie in any one group, and exactly 6 in some group.
All inputs are finite; a program needn't handle non-finite values.
Results may differ from a plain program's by a relative error of at most 0.00007.
Values sent between devices are 32-bit elements; how exact they have to be, the bound alone decides.
A program may use at most 128 MiB of HBM per device.

v0:
```python
import jax
import jax.numpy as jnp
from jax import lax
from jax.sharding import PartitionSpec as P


def split_up(array, dim, devices):
    before, after = (array.shape[:dim], array.shape[dim + 1 :])
    return jnp.moveaxis(array.reshape(*before, devices, -1, *after), dim, 0)


def piece_ends(length, count):
    turn = length // count
    if turn >= 8:
        turn -= turn % 8
    return [turn * k for k in range(1, count)]


def in_order(blocks, dim):
    blocks = jnp.moveaxis(blocks, 0, dim)
    lengths = blocks.shape
    return blocks.reshape(*lengths[:dim], lengths[dim] * lengths[dim + 1], *lengths[dim + 2 :])


def exchange_in_pieces(array, axis, pieces, split_dim, concat_dim):
    blocks = split_up(array, split_dim, lax.axis_size(axis))
    split_at = max(range(1, max(2, blocks.ndim - 1)), key=lambda d: blocks.shape[d])
    finished = []
    for share in jnp.split(blocks, piece_ends(blocks.shape[split_at], pieces), axis=split_at):
        if share.size:
            finished.append(lax.all_to_all(share, axis, split_axis=0, concat_axis=0, tiled=True))
    return in_order(jnp.concatenate(finished, axis=split_at), concat_dim)


def local(half_integrals, virtual_orbitals, occupied_energy, virtual_energy, partners):
    highest = lax.Precision.HIGHEST
    groups = lax.axis_size("occ")
    my_group = lax.axis_index("occ")
    my_column = lax.axis_index("aux")
    group_size = half_integrals.shape[1]
    pair_count = partners.shape[1]
    requests = group_size * pair_count
    capacity = requests // groups + 2
    working = jnp.einsum("qim,mv->qiv", half_integrals, virtual_orbitals, precision=highest)
    row_width = working.shape[2]
    slices = working.shape[0]
    source_group = (partners // group_size).reshape(groups, requests)
    local_index = (partners % group_size).reshape(groups, requests)
    request_ids = jnp.arange(requests, dtype=jnp.int32)
    earlier = request_ids[:, None] > request_ids[None, :]
    same_source = source_group[:, :, None] == source_group[:, None, :]
    slot_rank = jnp.sum((same_source & earlier[None]).astype(jnp.int32), axis=2)
    outgoing = (source_group == my_group).astype(jnp.int32)
    slot_ids = jnp.arange(capacity, dtype=jnp.int32)
    slot_match = outgoing[:, None, :] * (slot_rank[:, None, :] == slot_ids[None, :, None]).astype(
        jnp.int32
    )
    chosen = jnp.sum(slot_match * local_index[:, None, :], axis=2).reshape(-1)
    filled = jnp.sum(slot_match, axis=2).reshape(-1)
    outbound = jnp.take(working, chosen, axis=1) * filled.astype(working.dtype)[None, :, None]
    outbound = outbound.reshape(slices, groups, capacity, row_width)
    inbound = lax.all_to_all(outbound, "occ", split_axis=1, concat_axis=1, tiled=True)
    my_sources = lax.dynamic_index_in_dim(source_group, my_group, 0, keepdims=False)
    my_ranks = lax.dynamic_index_in_dim(slot_rank, my_group, 0, keepdims=False)
    partner_rows = jnp.take(
        inbound.reshape(slices, groups * capacity, row_width),
        my_sources * capacity + my_ranks,
        axis=1,
    )
    partner_rows = partner_rows.reshape(slices, group_size, pair_count, row_width)
    per_device = group_size // lax.axis_size("aux")
    first_orbital = my_group * group_size + my_column * per_device
    own_energy = lax.dynamic_slice_in_dim(occupied_energy, first_orbital, per_device, 0)
    own_partners = lax.dynamic_slice_in_dim(partners, first_orbital, per_device, 0)
    orbital_ids = jnp.arange(occupied_energy.shape[0], dtype=jnp.int32)
    partner_energy = jnp.sum(
        jnp.where(
            own_partners[:, :, None] == orbital_ids[None, None, :],
            occupied_energy[None, None, :],
            jnp.float32(0.0),
        ),
        axis=2,
    )
    pair_energy = (
        jnp.concatenate([own_energy[:, None], partner_energy], axis=1) + own_energy[:, None]
    )
    denominator = (
        virtual_energy[None, None, :, None]
        + virtual_energy[None, None, None, :]
        - pair_energy[:, :, None, None]
    )
    own_rows = exchange_in_pieces(working, "aux", 2, 1, 0)
    self_ints = jnp.einsum("qda,qdb->dab", own_rows, own_rows, precision=highest)
    self_amplitude = self_ints / denominator[:, 0]
    self_term = jnp.einsum("dab,qdb->qda", self_amplitude, own_rows, precision=highest)
    member_rows = lax.all_to_all(partner_rows, "aux", split_axis=1, concat_axis=0, tiled=True)
    cross_ints = jnp.einsum("qda,qdkb->dkab", own_rows, member_rows, precision=highest)
    cross_amplitude = cross_ints / denominator[:, 1:]
    gathered = self_term + jnp.einsum(
        "dkab,qdkb->qda", cross_amplitude, member_rows, precision=highest
    )
    return lax.all_to_all(gathered, "aux", split_axis=0, concat_axis=1, tiled=True)


def solution(mesh):
    return jax.shard_map(
        local,
        mesh=mesh,
        in_specs=(P("aux", "occ", None), P(), P(), P(), P()),
        out_specs=P("aux", "occ", None),
        check_vma=False,
    )
```

profile of v0, /device:TPU:2, one launch (start us, length us, event | category | flops | bytes accessed | tf_op | source)
XLA Modules:
  0.0 455.3 jit_solution(16977519400593986430)
XLA Ops:
  0.0 0.0 copy-start
  0.0 1.4 copy-done
  1.4 12.3 %fusion.3 = f32[64,32,512]{2,1,0:T(8,128)S(1)} fusion(f32[64,32,768]{2,1,0:T(8,128)} %param.5, f32[768,512]{1,0:T(8,128)S(1)} %copy-done), kind=kOutput, calls=%fused_computation.11 | convolution fusion | flops 9663676416 | bytes 12058624 | tf_op jit(solution)/shard_map/qim,mv->qiv/dot_general | solution.py:44
  13.7 0.0 copy-start.3
  13.7 2.3 fusion.22
  16.1 0.3 copy-done.3
  16.4 2.5 copy.20
  18.9 11.7 %all-to-all-start = ((f32[32,32,1,512]{3,1,2,0:T(8,128)}), f32[32,32,1,512]{3,1,2,0:T(8,128)}, u32[]{:S(2)}, u32[]{:S(2)}) async-start(f32[32,32,1,512]{3,1,2,0:T(8,128)} %copy.20), calls=%async_computation | async-start | bytes 4194304 | tf_op jit(solution)/shard_map/all_to_all | solution.py:31
  30.6 0.0 copy-start.7
  30.6 6.6 %copy.27 = f32[64,32,512]{2,0,1:T(8,128)} copy(f32[64,32,512]{2,1,0:T(8,128)} %copy-done.3) | data formatting | bytes 8388608 | tf_op jit(solution)/shard_map/qim,mv->qiv/dot_general | solution.py:44
  37.2 0.0 copy-done.7
  37.2 0.1 reshape.243
  37.3 0.1 mul.52
  37.4 0.3 convert_reduce_fusion
  37.7 0.3 select_reduce_fusion
  38.0 0.1 copy.26
  38.1 0.1 reshape.244
  38.2 0.1 copy.25
  38.3 0.1 copy.28
  38.4 5.8 %gather_fusion = f32[48,64,512]{2,1,0:T(8,128)} fusion(f32[64,32,512]{2,0,1:T(8,128)} %copy.27, s32[1024]{0:T(1024)S(1)} %pad_clamp_fusion.1), kind=kCustom, calls=%fused_computation | custom fusion | bytes 12583104 | tf_op jit(solution)/shard_map/jit(_take)/gather | solution.py:60
  44.2 6.9 %select_multiply_fusion = f32[64,8,6,512]{3,0,2,1:T(8,128)} fusion(f32[64,8,6,512]{3,0,2,1:T(8,128)} %bitcast.78, f32[8,6]{1,0:T(8,128)S(1)} %copy.28, pred[8,6]{1,0:T(8,128)(4,1)S(1)} %copy.25), kind=kLoop, calls=%fused_computation.2 | loop fusion | flops 3145728 | bytes 12583152 | tf_op jit(solution)/shard_map/mul | solution.py:60
  51.1 28.8 %all-to-all-done = f32[32,32,1,512]{3,1,2,0:T(8,128)} async-done(((f32[32,32,1,512]{3,1,2,0:T(8,128)}), f32[32,32,1,512]{3,1,2,0:T(8,128)}, u32[]{:S(2)}, u32[]{:S(2)}) %all-to-all-start) | async-done | bytes 2097184 | tf_op jit(solution)/shard_map/all_to_all | solution.py:31
  79.9 15.5 %all-to-all-start.2 = ((f32[64,8,6,512]{3,0,2,1:T(8,128)}), f32[64,8,6,512]{3,0,2,1:T(8,128)}, u32[]{:S(2)}, u32[]{:S(2)}) async-start(f32[64,8,6,512]{3,0,2,1:T(8,128)} %select_multiply_fusion), calls=%async_computation.2 | async-start | bytes 12582912 | tf_op jit(solution)/shard_map/all_to_all | solution.py:62
  95.4 4.1 copy.21
  99.5 68.0 %all-to-all-done.2 = f32[64,8,6,512]{3,0,2,1:T(8,128)} async-done(((f32[64,8,6,512]{3,0,2,1:T(8,128)}), f32[64,8,6,512]{3,0,2,1:T(8,128)}, u32[]{:S(2)}, u32[]{:S(2)}) %all-to-all-start.2) | async-done | bytes 6291488 | tf_op jit(solution)/shard_map/all_to_all | solution.py:62
  167.5 6.9 %all-to-all-start.1 = ((f32[32,32,1,512]{3,1,2,0:T(8,128)}), f32[32,32,1,512]{3,1,2,0:T(8,128)}, u32[]{:S(2)}, u32[]{:S(2)}) async-start(f32[32,32,1,512]{3,1,2,0:T(8,128)} %copy.21), calls=%async_computation.1 | async-start | bytes 4194304 | tf_op jit(solution)/shard_map/all_to_all | solution.py:31
  174.5 5.6 %gather_fusion.1 = f32[32,64,512]{2,1,0:T(8,128)} fusion(f32[64,48,512]{2,0,1:T(8,128)} %bitcast.15, s32[1024]{0:T(1024)S(1)} %pad_clamp_fusion), kind=kCustom, calls=%fused_computation.1 | custom fusion | bytes 8388736 | tf_op jit(solution)/shard_map/jit(_take)/gather | solution.py:65
  180.1 5.0 %fusion = f32[64,32,1,512]{3,0,2,1:T(8,128)} fusion(f32[32,64,512]{2,1,0:T(8,128)} %gather_fusion.1, pred[32]{0:T(512)(128)(4,1)S(1)} %get-tuple-element.9), kind=kLoop, calls=%fused_computation.4 | loop fusion | flops 1048576 | bytes 8388640 | tf_op jit(solution)/shard_map/jit(_take)/select_n | solution.py:65
  185.1 0.0 copy-start.8
  185.1 0.0 copy-start.6
  185.1 38.5 %all-to-all-done.1 = f32[32,32,1,512]{3,1,2,0:T(8,128)} async-done(((f32[32,32,1,512]{3,1,2,0:T(8,128)}), f32[32,32,1,512]{3,1,2,0:T(8,128)}, u32[]{:S(2)}, u32[]{:S(2)}) %all-to-all-start.1) | async-done | bytes 2097184 | tf_op jit(solution)/shard_map/all_to_all | solution.py:31
  223.6 6.9 %all-to-all-start.3 = ((f32[64,32,1,512]{3,0,2,1:T(8,128)}), f32[64,32,1,512]{3,0,2,1:T(8,128)}, u32[]{:S(2)}, u32[]{:S(2)}) async-start(f32[64,32,1,512]{3,0,2,1:T(8,128)} %fusion), calls=%async_computation.3 | async-start | bytes 8388608 | tf_op jit(solution)/shard_map/all_to_all | solution.py:96
  230.5 0.6 constant_dynamic-slice_fusion.2
  231.0 0.0 copy-done.8
  231.0 0.6 dynamic_slice.13
  231.7 1.2 fusion.14
  232.9 2.0 maximum_add_fusion
  234.9 0.0 copy-done.6
  234.9 0.1 broadcast_add_fusion
  235.0 0.3 broadcast_subtract_fusion
  235.4 0.0 copy-start.5
  235.4 3.6 copy_dynamic-update-slice_fusion.1
  238.9 2.8 copy_dynamic-update-slice_fusion
  241.7 2.4 copy.24
  244.2 0.0 copy-done.5
  244.2 0.0 copy-start.2
  244.2 7.0 %fusion.8 = f32[512,512]{1,0:T(8,128)S(1)} fusion(f32[32,64,1,512]{3,0,1,2:T(8,128)S(1)} %copy_dynamic-update-slice_fusion, f32[1,2,512,512]{3,2,1,0:T(8,128)S(1)} %broadcast_subtract_fusion), kind=kOutput, calls=%fused_computation.15 | convolution fusion | flops 6442713088 | bytes 6291456 | tf_op jit(solution)/shard_map/qda,qdb->dab/dot_general | solution.py:93
  251.2 0.0 copy-done.2
  251.2 8.3 %fusion.23 = f32[2048,512]{1,0:T(8,128)} fusion(f32[2048,512]{1,0:T(8,128)S(1)} %bitcast.75, f32[512,512]{1,0:T(8,128)S(1)} %fusion.8), kind=kOutput, calls=%fused_computation.54 | convolution fusion | flops 6442450944 | bytes 9437184 | tf_op jit(solution)/shard_map/dab,qdb->qda/dot_general | solution.py:95
  259.5 63.2 %all-to-all-done.3 = f32[64,32,1,512]{3,0,2,1:T(8,128)} async-done(((f32[64,32,1,512]{3,0,2,1:T(8,128)}), f32[64,32,1,512]{3,0,2,1:T(8,128)}, u32[]{:S(2)}, u32[]{:S(2)}) %all-to-all-start.3) | async-done | bytes 4194336 | tf_op jit(solution)/shard_map/all_to_all | solution.py:96
  322.7 0.0 copy-start.4
  322.7 9.9 %fusion.12 = f32[512,512]{1,0:T(8,128)S(1)} fusion(f32[2048,512]{1,0:T(8,128)} %bitcast.23, f32[2048,512]{1,0:T(8,128)} %bitcast.76, f32[1,2,512,512]{3,2,1,0:T(8,128)} %copy-done.5), kind=kOutput, calls=%fused_computation.17 | convolution fusion | flops 6442713088 | bytes 10485760 | tf_op jit(solution)/shard_map/qda,qdkb->dkab/dot_general | solution.py:97
  332.6 0.0 copy-done.4
  332.6 8.6 %add_bitcast_fusion = f32[2048,1,512]{2,0,1:T(8,128)S(1)} fusion(f32[2048,512]{1,0:T(8,128)S(1)} %copy-done.4, f32[2048,512]{1,0:T(8,128)} %bitcast.23, f32[512,512]{1,0:T(8,128)S(1)} %fusion.12), kind=kOutput, calls=%fused_computation.8 | convolution fusion | flops 6443499520 | bytes 13631488 | tf_op jit(solution)/shard_map/dkab,qdkb->qda/dot_general | solution.py:99
  341.2 8.0 %copy.31 = f32[2048,1,512]{2,1,0:T(1,128)S(1)} copy(f32[2048,1,512]{2,0,1:T(8,128)S(1)} %add_bitcast_fusion) | data formatting | bytes 8388608 | tf_op jit(solution)/shard_map/add | solution.py:99
  349.2 101.2 %all_to_all.48 = f32[2048,1,512]{2,1,0:T(1,128)S(1)} all-to-all(f32[2048,1,512]{2,1,0:T(1,128)S(1)} %copy.31), channel_id=1, replica_groups=mesh['aux'=32,'occ'=8] {'aux'}, dimensions={0} | all-to-all | bytes 8388608 | tf_op jit(solution)/shard_map/all_to_all | solution.py:102
  450.4 0.0 copy-start.1
  450.4 4.4 copy.37
  454.8 0.0 copy-done.1
  (10 shorter events, 0.1 us)
Async XLA Ops:
  0.0 1.4 copy-start
  13.7 2.7 copy-start.3
  18.9 61.0 %all-to-all-start = ((f32[32,32,1,512]{3,1,2,0:T(8,128)}), f32[32,32,1,512]{3,1,2,0:T(8,128)}, u32[]{:S(2)}, u32[]{:S(2)}) async-start(f32[32,32,1,512]{3,1,2,0:T(8,128)} %copy.20), calls=%async_computation | async-start | bytes 4194304 | tf_op jit(solution)/shard_map/all_to_all | solution.py:31
  30.6 6.6 %copy-start.7 = (s32[256,1]{0,1:T(1,128)S(1)}, s32[256,1]{0,1:T(1,128)}, u32[]{:S(2)}) copy-start(s32[256,1]{0,1:T(1,128)} %param.9) | copy-start | bytes 3076
  79.9 87.6 %all-to-all-start.2 = ((f32[64,8,6,512]{3,0,2,1:T(8,128)}), f32[64,8,6,512]{3,0,2,1:T(8,128)}, u32[]{:S(2)}, u32[]{:S(2)}) async-start(f32[64,8,6,512]{3,0,2,1:T(8,128)} %select_multiply_fusion), calls=%async_computation.2 | async-start | bytes 12582912 | tf_op jit(solution)/shard_map/all_to_all | solution.py:62
  167.5 56.0 %all-to-all-start.1 = ((f32[32,32,1,512]{3,1,2,0:T(8,128)}), f32[32,32,1,512]{3,1,2,0:T(8,128)}, u32[]{:S(2)}, u32[]{:S(2)}) async-start(f32[32,32,1,512]{3,1,2,0:T(8,128)} %copy.21), calls=%async_computation.1 | async-start | bytes 4194304 | tf_op jit(solution)/shard_map/all_to_all | solution.py:31
  185.1 46.0 %copy-start.8 = (f32[256]{0:T(256)S(1)}, f32[256]{0:T(256)}, u32[]{:S(2)}) copy-start(f32[256]{0:T(256)} %param.7) | copy-start | bytes 3076
  185.1 49.8 %copy-start.6 = (f32[512]{0:T(512)S(1)}, f32[512]{0:T(512)}, u32[]{:S(2)}) copy-start(f32[512]{0:T(512)} %param.8) | copy-start | bytes 6148
  223.6 99.2 %all-to-all-start.3 = ((f32[64,32,1,512]{3,0,2,1:T(8,128)}), f32[64,32,1,512]{3,0,2,1:T(8,128)}, u32[]{:S(2)}, u32[]{:S(2)}) async-start(f32[64,32,1,512]{3,0,2,1:T(8,128)} %fusion), calls=%async_computation.3 | async-start | bytes 8388608 | tf_op jit(solution)/shard_map/all_to_all | solution.py:96
  235.4 8.8 %copy-start.5 = (f32[1,2,512,512]{3,2,1,0:T(8,128)}, f32[1,2,512,512]{3,2,1,0:T(8,128)S(1)}, u32[]{:S(2)}) copy-start(f32[1,2,512,512]{3,2,1,0:T(8,128)S(1)} %broadcast_subtract_fusion) | copy-start | bytes 6291460
  244.2 7.0 %copy-start.2 = (f32[32,64,1,512]{3,1,0,2:T(8,128)}, f32[32,64,1,512]{3,1,0,2:T(8,128)S(1)}, u32[]{:S(2)}) copy-start(f32[32,64,1,512]{3,1,0,2:T(8,128)S(1)} %copy.24) | copy-start | bytes 12582916
  322.7 9.9 %copy-start.4 = (f32[2048,512]{1,0:T(8,128)S(1)}, f32[2048,512]{1,0:T(8,128)}, u32[]{:S(2)}) copy-start(f32[2048,512]{1,0:T(8,128)} %fusion.23) | copy-start | bytes 12582916
  450.4 4.4 copy-start.1
where the time goes:
time: 464 us; the launch traced here: 455 us
  waiting for transfers between devices  199 us (43%)
  blocking collectives  101 us (22%)
  local copies, waits for them, and re-layouts  51.8 us (11%)
  matrix products  46 us (10%)
  starting transfers between devices  40.9 us (9%)
  other arithmetic  16.2 us (3%)
    all_to_all x1, blocking collectives, local(): lax.all_to_all(gathered, 'aux', split_axis=0, concat_axis=1, tiled=True)  101 us
    all_to_all x1, waiting for transfers between devices, local(): lax.all_to_all(outbound, 'occ', split_axis=1, concat_axis=1, tiled=True)  68 us
    all_to_all x2, waiting for transfers between devices, exchange_in_pieces(): lax.all_to_all(share, axis, split_axis=0, concat_axis=0, tiled=True)  67.3 us
    all_to_all x1, waiting for transfers between devices, local(): lax.all_to_all(partner_rows, 'aux', split_axis=1, concat_axis=0, tiled=True)  63.2 us
    all_to_all x2, starting transfers between devices, exchange_in_pieces(): lax.all_to_all(share, axis, split_axis=0, concat_axis=0, tiled=True)  18.6 us
    all_to_all x1, starting transfers between devices, local(): lax.all_to_all(outbound, 'occ', split_axis=1, concat_axis=1, tiled=True)  15.5 us
    dot_general x1, matrix products, local(): jnp.einsum('qim,mv->qiv', half_integrals, virtual_orbitals, precision=hig...  12.3 us
    dot_general x1, matrix products, local(): jnp.einsum('qda,qdkb->dkab', own_rows, member_rows, precision=highest)  9.86 us
  transfers between devices with their start and end apart: 4, of which 4 were waited for; matrix products, arithmetic and copies ran while one was open for 14% of the time, Pallas kernels for 0%

commit v1 on v0

v1 whole, which is shorter than its diff:
```python
import jax
import jax.numpy as jnp
from jax import lax
from jax.experimental import pallas as pl
from jax.experimental.pallas import tpu as pltpu
from jax.sharding import PartitionSpec as P

CAPACITY = 6


def take_rows_kernel(rows_ref, x_ref, o_ref):
    o_ref[...] = x_ref[...]


def take_rows(x, rows):
    count = rows.shape[0]
    block = (1,) + x.shape[1:]
    return pl.pallas_call(
        take_rows_kernel,
        out_shape=jax.ShapeDtypeStruct((count,) + x.shape[1:], x.dtype),
        grid_spec=pltpu.PrefetchScalarGridSpec(
            num_scalar_prefetch=1,
            grid=(count,),
            in_specs=[pl.BlockSpec(block, lambda i, r: (r[i], 0, 0))],
            out_specs=pl.BlockSpec(block, lambda i, r: (i, 0, 0)),
        ),
        cost_estimate=pl.CostEstimate(flops=0, bytes_accessed=2 * count * x[0].size * 4, transcendentals=0),
    )(rows, x)


def local(half_integrals, virtual_orbitals, occupied_energy, virtual_energy, partners):
    high = lax.Precision.HIGH
    groups = lax.axis_size("occ")
    columns = lax.axis_size("aux")
    me = lax.axis_index("occ")
    column = lax.axis_index("aux")
    slices, size, _ = half_integrals.shape
    width = virtual_orbitals.shape[1]
    table = partners.reshape(groups, size)
    source = table // size
    index = table % size
    ids = jnp.arange(size, dtype=jnp.int32)
    same = source[:, :, None] == source[:, None, :]
    rank = jnp.sum((same & (ids[:, None] > ids[None, :])[None]).astype(jnp.int32), axis=2)
    slots = jnp.arange(CAPACITY, dtype=jnp.int32)
    match = (source == me)[:, None, :] & (rank[:, None, :] == slots[None, :, None])
    chosen = jnp.sum(jnp.where(match, index[:, None, :], 0), axis=2)
    my_source = lax.dynamic_index_in_dim(source, me, 0, keepdims=False)
    my_rank = lax.dynamic_index_in_dim(rank, me, 0, keepdims=False)
    my_place = lax.rem(my_source - me + groups, groups) * CAPACITY + my_rank

    rows = jnp.einsum("qim,mv->iqv", half_integrals, virtual_orbitals, precision=high)
    received = []
    order = lax.rem(me + jnp.arange(groups, dtype=jnp.int32), groups)
    outbound = take_rows(rows, jnp.take_along_axis(chosen, order[:, None], axis=0).reshape(-1))
    outbound = outbound.reshape(groups, CAPACITY, slices, width)
    own = lax.all_to_all(rows, "aux", split_axis=0, concat_axis=0, tiled=True)
    received = [outbound[0]]
    for d in range(1, groups):
        received.append(
            lax.ppermute(outbound[d], "occ", [(g, (g + d) % groups) for g in range(groups)])
        )
    pieces = jnp.stack([received[(groups - d) % groups] for d in range(groups)])
    partner_rows = take_rows(pieces.reshape(groups * CAPACITY, slices, width), my_place)
    member = lax.all_to_all(partner_rows, "aux", split_axis=0, concat_axis=0, tiled=True)

    first = me * size + column
    orbital_ids = jnp.arange(groups * size, dtype=jnp.int32)
    pick = lambda i: jnp.sum(jnp.where(orbital_ids == i, occupied_energy, jnp.float32(0.0)))
    own_partner = jnp.sum(jnp.where(orbital_ids == first, partners[:, 0], 0))
    own_energy = pick(first)
    partner_energy = pick(own_partner)
    virtual_pair = virtual_energy[:, None] + virtual_energy[None, :]
    own = own.reshape(columns * slices, width)
    member = member.reshape(columns * slices, width)
    self_t = jnp.einsum("qb,qa->ba", own, own, precision=high) / (virtual_pair - (own_energy + own_energy))
    self_term = jnp.einsum("qb,ba->qa", own, self_t, precision=high)
    cross_t = jnp.einsum("qb,qa->ba", member, own, precision=high) / (virtual_pair - (own_energy + partner_energy))
    density = self_term + jnp.einsum("qb,ba->qa", member, cross_t, precision=high)
    density = lax.all_to_all(
        density.reshape(columns, slices, width), "aux", split_axis=0, concat_axis=0, tiled=True
    )
    return jnp.transpose(density, (1, 0, 2))


def solution(mesh):
    return jax.shard_map(
        local,
        mesh=mesh,
        in_specs=(P("aux", "occ", None), P(), P(), P(), P()),
        out_specs=P("aux", "occ", None),
        check_vma=False,
    )
```

time: 464 us -> 387 us (0.83)
  waiting for transfers between devices: 199 us -> 129 us
  Pallas kernels: 0 us -> 45.2 us
  local copies, waits for them, and re-layouts: 51.8 us -> 22.9 us
  other arithmetic: 16.2 us -> 3.73 us
  starting transfers between devices: 40.9 us -> 30.7 us
    all_to_all x4 -> x2, waiting for transfers between devices: 199 us -> 69.4 us  [the longest x1 69.4 us: local(): lax.all_to_all(partner_rows, 'aux', split_axis=0, concat_axis=0, tiled=True)]
    ppermute x0 -> x7, waiting for transfers between devices: none -> 59.6 us  [local(): lax.ppermute(outbound[d], 'occ', [(g, (g + d) % groups) for g in range(gr...]
    pallas_call x0 -> x2, Pallas kernels: none -> 45.2 us  [take_rows(): pl.pallas_call(take_rows_kernel, out_shape=jax.ShapeDtypeStruct((count,)...]
    all_to_all x4 -> x2, starting transfers between devices: 40.9 us -> 23.4 us  [the longest x1 11.8 us: local(): own = lax.all_to_all(rows, 'aux', split_axis=0, concat_axis=0, tiled=True)]
    gather x2 -> x1, local copies, waits for them, and re-layouts: 11.4 us -> 0.56 us  [local(): jnp.take_along_axis(chosen, order[:, None], axis=0).reshape(-1)]
    split x3 -> x0, local copies, waits for them, and re-layouts: 9.03 us -> none  [exchange_in_pieces(): jnp.split(blocks, piece_ends(blocks.shape[split_at], pieces), axis=split_at)]
    add x1 -> x0, local copies, waits for them, and re-layouts: 8.01 us -> none  [local(): self_term + jnp.einsum('dkab,qdkb->qda', cross_amplitude, member_rows, pr...]
    ppermute x0 -> x7, starting transfers between devices: none -> 7.24 us  [local(): lax.ppermute(outbound[d], 'occ', [(g, (g + d) % groups) for g in range(gr...]
  transfers between devices with their start and end apart: 4 -> 9, of which waited for: 4 -> 6; matrix products, arithmetic and copies ran while one was open for 14% -> 10% of each run, Pallas kernels for 0% -> 12%
where the time goes in v1:
time: 387 us; the launch traced here: 382 us
  waiting for transfers between devices  129 us (33%)
  blocking collectives  98.6 us (25%)
  matrix products  49.3 us (13%)
  Pallas kernels  45.2 us (12%)
  starting transfers between devices  30.7 us (8%)
  local copies, waits for them, and re-layouts  22.9 us (6%)
    all_to_all x1, blocking collectives, local(): lax.all_to_all(density.reshape(columns, slices, width), 'aux', split_axis...  98.6 us
    all_to_all x1, waiting for transfers between devices, local(): lax.all_to_all(partner_rows, 'aux', split_axis=0, concat_axis=0, tiled=True)  69.4 us
    ppermute x7, waiting for transfers between devices, local(): lax.ppermute(outbound[d], 'occ', [(g, (g + d) % groups) for g in range(gr...  59.6 us
    pallas_call x2, Pallas kernels, take_rows(): pl.pallas_call(take_rows_kernel, out_shape=jax.ShapeDtypeStruct((count,)...  45.2 us
    dot_general x1, matrix products, local(): jnp.einsum('qim,mv->iqv', half_integrals, virtual_orbitals, precision=high)  15.9 us
    all_to_all x1, starting transfers between devices, local(): own = lax.all_to_all(rows, 'aux', split_axis=0, concat_axis=0, tiled=True)  11.8 us
    all_to_all x1, starting transfers between devices, local(): lax.all_to_all(partner_rows, 'aux', split_axis=0, concat_axis=0, tiled=True)  11.6 us
    unnamed x20, local copies, waits for them, and re-layouts  11.1 us
  transfers between devices with their start and end apart: 9, of which 6 were waited for; matrix products, arithmetic and copies ran while one was open for 10% of the time, Pallas kernels for 12%

profile of v1, /device:TPU:2, one launch (start us, length us, event | category | flops | bytes accessed | tf_op | source)
XLA Modules:
  0.0 381.7 jit_solution(6437244828316777726)
XLA Ops:
  0.0 0.0 copy-start
  0.0 1.4 copy-done
  1.4 15.9 %fusion.2.x_ref = f32[32,64,512]{2,1,0:T(8,128)} fusion(f32[64,32,768]{2,1,0:T(8,128)} %param.5, f32[768,512]{1,0:T(8,128)S(1)} %copy-done), kind=kOutput, calls=%fused_computation.4 | convolution fusion | flops 4831838208 | bytes 12058624 | tf_op jit(solution)/shard_map/qim,mv->iqv/dot_general | solution.py:52
  17.3 0.0 copy-start.3
  17.3 11.8 %all-to-all-start = ((f32[32,64,512]{2,1,0:T(8,128)}), f32[32,64,512]{2,1,0:T(8,128)}, u32[]{:S(2)}, u32[]{:S(2)}) async-start(f32[32,64,512]{2,1,0:T(8,128)} %fusion.2.x_ref), calls=%async_computation | async-start | bytes 8388608 | tf_op jit(solution)/shard_map/all_to_all | solution.py:57
  29.1 0.6 broadcast.210
  29.7 0.0 copy-done.3
  29.7 0.6 reduce.3
  30.3 0.1 reshape.185
  30.4 0.3 convert_reduce_fusion
  30.8 0.2 select_reduce_fusion
  30.9 0.1 copy.11
  31.0 0.6 gather_fusion
  31.6 0.1 broadcast_select_fusion
  31.7 0.6 select_n.79.rows_ref
  32.3 26.7 %shard_map.55 = f32[48,64,512]{2,1,0:T(8,128)} custom-call(s32[48]{0:T(128)} %select_n.79.rows_ref, f32[32,64,512]{2,1,0:T(8,128)} %fusion.2.x_ref), custom_call_target="tpu_custom_call" | custom-call | bytes 12582912 | tf_op jit(solution)/shard_map/pallas_call | solution.py:18
  59.0 5.0 %fusion.19 = (f32[6,64,512]{2,1,0:T(8,128)}, f32[6,64,512]{2,1,0:T(8,128)}, f32[6,64,512]{2,1,0:T(8,128)}, f32[6,64,512]{2,1,0:T(8,128)}, f32[6,64,512]{2,1,0:T(...) fusion(f32[48,64,512]{2,1,0:T(8,128)} %shard_map.55), kind=kLoop, calls=%fused_computation.57 | loop fusion | bytes 11010048 | tf_op jit(solution)/shard_map/slice | solution.py:61
  64.0 1.8 collective-permute-start
  65.8 1.3 collective-permute-start.1
  67.2 0.5 collective-permute-start.2
  67.6 2.9 collective-permute-start.3
  70.5 0.0 collective-permute-start.4
  70.5 0.6 fusion.15.rows_ref
  71.1 2.1 fusion.8
  73.2 10.0 %collective-permute-done = f32[6,64,512]{2,1,0:T(8,128)} collective-permute-done((f32[6,64,512]{2,1,0:T(8,128)}, f32[6,64,512]{2,1,0:T(8,128)}, u32[]{:S(2)}, u32[]{:S(2)}) %collective-permute-start) | collective-permute-done | bytes 786464 | tf_op jit(solution)/shard_map/ppermute | solution.py:61
  83.2 0.7 collective-permute-start.5
  84.0 2.1 bitcast_dynamic-update-slice_fusion.6
  86.1 15.1 %collective-permute-done.1 = f32[6,64,512]{2,1,0:T(8,128)S(1)} collective-permute-done((f32[6,64,512]{2,1,0:T(8,128)}, f32[6,64,512]{2,1,0:T(8,128)S(1)}, u32[]{:S(2)}, u32[]{:S(2)}) %collective-permute-start.1) | collective-permute-done | bytes 786464 | tf_op jit(solution)/shard_map/ppermute | solution.py:61
  101.2 0.0 collective-permute-start.6
  101.2 1.0 bitcast_dynamic-update-slice_fusion.5
  102.2 0.0 collective-permute-done.2
  102.2 1.0 bitcast_dynamic-update-slice_fusion.4
  103.2 2.8 collective-permute-done.3
  106.0 1.0 bitcast_dynamic-update-slice_fusion.3
  107.0 11.1 %collective-permute-done.4 = f32[6,64,512]{2,1,0:T(8,128)S(1)} collective-permute-done((f32[6,64,512]{2,1,0:T(8,128)}, f32[6,64,512]{2,1,0:T(8,128)S(1)}, u32[]{:S(2)}, u32[]{:S(2)}) %collective-permute-start.4) | collective-permute-done | bytes 786464 | tf_op jit(solution)/shard_map/ppermute | solution.py:61
  118.1 1.0 bitcast_dynamic-update-slice_fusion.2
  119.1 20.5 %collective-permute-done.5 = f32[6,64,512]{2,1,0:T(8,128)S(1)} collective-permute-done((f32[6,64,512]{2,1,0:T(8,128)}, f32[6,64,512]{2,1,0:T(8,128)S(1)}, u32[]{:S(2)}, u32[]{:S(2)}) %collective-permute-start.5) | collective-permute-done | bytes 786464 | tf_op jit(solution)/shard_map/ppermute | solution.py:61
  139.6 0.9 bitcast_dynamic-update-slice_fusion.1
  140.5 0.0 collective-permute-done.6
  140.5 0.9 bitcast_dynamic-update-slice_fusion
  141.5 18.5 %shard_map.56 = f32[32,64,512]{2,1,0:T(8,128)} custom-call(s32[32]{0:T(128)} %fusion.15.rows_ref, f32[48,64,512]{2,1,0:T(8,128)} %bitcast.15.x_ref), custom_call_target="tpu_custom_call" | custom-call | bytes 8388608 | tf_op jit(solution)/shard_map/pallas_call | solution.py:18
  160.0 0.0 copy-start.4
  160.0 0.0 copy-start.5
  160.0 0.0 all-to-all-done
  160.0 11.6 %all-to-all-start.1 = ((f32[32,64,512]{2,1,0:T(8,128)}), f32[32,64,512]{2,1,0:T(8,128)}, u32[]{:S(2)}, u32[]{:S(2)}) async-start(f32[32,64,512]{2,1,0:T(8,128)} %shard_map.56), calls=%async_computation.1 | async-start | bytes 8388608 | tf_op jit(solution)/shard_map/all_to_all | solution.py:65
  171.7 0.6 select_reduce_fusion.1
  172.3 0.0 copy-done.4
  172.3 1.3 fusion.12
  175.8 0.0 copy-done.5
  175.8 10.4 %fusion.6 = f32[512,512]{1,0:T(8,128)S(1)} fusion(f32[32,64,512]{2,1,0:T(8,128)} %all-to-all-done, f32[]{:T(128)S(6)} %add.100, f32[512]{0:T(512)S(1)} %copy-done.5), kind=kOutput, calls=%fused_computation.10 | convolution fusion | flops 3222011904 | bytes 5244932 | tf_op jit(solution)/shard_map/qb,qa->ba/dot_general | solution.py:76
  186.3 7.2 %fusion.20 = f32[2048,512]{1,0:T(8,128)} fusion(f32[2048,512]{1,0:T(8,128)} %bitcast.2, f32[512,512]{1,0:T(8,128)S(1)} %fusion.6), kind=kOutput, calls=%fused_computation.58 | convolution fusion | flops 3221225472 | bytes 9437184 | tf_op jit(solution)/shard_map/qb,ba->qa/dot_general | solution.py:77
  193.4 69.4 %all-to-all-done.1 = f32[32,64,512]{2,1,0:T(8,128)} async-done(((f32[32,64,512]{2,1,0:T(8,128)}), f32[32,64,512]{2,1,0:T(8,128)}, u32[]{:S(2)}, u32[]{:S(2)}) %all-to-all-start.1) | async-done | bytes 4194336 | tf_op jit(solution)/shard_map/all_to_all | solution.py:65
  262.8 0.0 copy-start.2
  262.8 10.5 %fusion.7 = f32[512,512]{1,0:T(8,128)S(1)} fusion(f32[32,64,512]{2,1,0:T(8,128)} %all-to-all-done.1, f32[32,64,512]{2,1,0:T(8,128)} %all-to-all-done, f32[]{:T(128)S(6)} %add.112, f32[512]{0:T(512)S(1)} %copy-done.5), kind=kOutput, calls=%fused_computation.11 | convolution fusion | flops 3222011904 | bytes 9439236 | tf_op jit(solution)/shard_map/qb,qa->ba/dot_general | solution.py:78
  273.4 0.0 copy-done.2
  273.4 5.3 %convolution_add_fusion = f32[2048,512]{1,0:T(8,128)S(1)} fusion(f32[2048,512]{1,0:T(8,128)S(1)} %copy-done.2, f32[2048,512]{1,0:T(8,128)} %bitcast.16, f32[512,512]{1,0:T(8,128)S(1)} %fusion.7), kind=kOutput, calls=%fused_computation.3 | convolution fusion | flops 3222274048 | bytes 13631488 | tf_op jit(solution)/shard_map/qb,ba->qa/dot_general | solution.py:79
  278.6 98.6 %all_to_all.15 = f32[32,64,512]{2,1,0:T(8,128)S(1)} all-to-all(f32[32,64,512]{2,1,0:T(8,128)S(1)} %bitcast.52), channel_id=1, replica_groups=mesh['aux'=32,'occ'=8] {'aux'}, dimensions={0} | all-to-all | bytes 8388608 | tf_op jit(solution)/shard_map/all_to_all | solution.py:80
  377.3 0.0 copy-start.1
  377.3 4.4 %copy.12 = f32[64,32,512]{2,1,0:T(8,128)} copy(f32[64,32,512]{2,0,1:T(8,128)S(1)} %bitcast.53) | data formatting | bytes 8388608 | tf_op jit(solution)/shard_map/transpose | solution.py:83
  381.7 0.0 copy-done.1
  (6 shorter events, 0.1 us)
Async XLA Ops:
  0.0 1.4 copy-start
  17.3 12.4 %copy-start.3 = (s32[256,1]{0,1:T(1,128)S(1)}, s32[256,1]{0,1:T(1,128)}, u32[]{:S(2)}) copy-start(s32[256,1]{0,1:T(1,128)} %param.9) | copy-start | bytes 3076
  17.3 142.7 %all-to-all-start = ((f32[32,64,512]{2,1,0:T(8,128)}), f32[32,64,512]{2,1,0:T(8,128)}, u32[]{:S(2)}, u32[]{:S(2)}) async-start(f32[32,64,512]{2,1,0:T(8,128)} %fusion.2.x_ref), calls=%async_computation | async-start | bytes 8388608 | tf_op jit(solution)/shard_map/all_to_all | solution.py:57
  64.0 19.2 %collective-permute-start = (f32[6,64,512]{2,1,0:T(8,128)}, f32[6,64,512]{2,1,0:T(8,128)}, u32[]{:S(2)}, u32[]{:S(2)}) collective-permute-start(f32[6,64,512]{2,1,0:T(8,128)} %get-tuple-element.15), channel_id=1, source_target_pairs={{0,7},{1,0},{2,1},{3,2},{4,3},{5,4},{6,5},{7,6},{8,15},{9,8},{10,9... | collective-permute-start | bytes 2359304 | tf_op jit(solution)/shard_map/ppermute | solution.py:61
  65.8 35.3 %collective-permute-start.1 = (f32[6,64,512]{2,1,0:T(8,128)}, f32[6,64,512]{2,1,0:T(8,128)S(1)}, u32[]{:S(2)}, u32[]{:S(2)}) collective-permute-start(f32[6,64,512]{2,1,0:T(8,128)} %get-tuple-element.14), channel_id=1, source_target_pairs={{0,6},{1,7},{2,0},{3,1},{4,2},{5,3},{6,4},{7,5},{8,14},{9,15},{10,... | collective-permute-start | bytes 2359304 | tf_op jit(solution)/shard_map/ppermute | solution.py:61
  67.2 35.0 %collective-permute-start.2 = (f32[6,64,512]{2,1,0:T(8,128)}, f32[6,64,512]{2,1,0:T(8,128)S(1)}, u32[]{:S(2)}, u32[]{:S(2)}) collective-permute-start(f32[6,64,512]{2,1,0:T(8,128)} %get-tuple-element.13), channel_id=1, source_target_pairs={{0,5},{1,6},{2,7},{3,0},{4,1},{5,2},{6,3},{7,4},{8,13},{9,14},{10,... | collective-permute-start | bytes 2359304 | tf_op jit(solution)/shard_map/ppermute | solution.py:61
  67.6 38.4 %collective-permute-start.3 = (f32[6,64,512]{2,1,0:T(8,128)}, f32[6,64,512]{2,1,0:T(8,128)S(1)}, u32[]{:S(2)}, u32[]{:S(2)}) collective-permute-start(f32[6,64,512]{2,1,0:T(8,128)} %get-tuple-element.12), channel_id=1, source_target_pairs={{0,4},{1,5},{2,6},{3,7},{4,0},{5,1},{6,2},{7,3},{8,12},{9,13},{10,... | collective-permute-start | bytes 2359304 | tf_op jit(solution)/shard_map/ppermute | solution.py:61
  70.5 47.6 %collective-permute-start.4 = (f32[6,64,512]{2,1,0:T(8,128)}, f32[6,64,512]{2,1,0:T(8,128)S(1)}, u32[]{:S(2)}, u32[]{:S(2)}) collective-permute-start(f32[6,64,512]{2,1,0:T(8,128)} %get-tuple-element.11), channel_id=1, source_target_pairs={{0,3},{1,4},{2,5},{3,6},{4,7},{5,0},{6,1},{7,2},{8,11},{9,12},{10,... | collective-permute-start | bytes 2359304 | tf_op jit(solution)/shard_map/ppermute | solution.py:61
  83.2 56.3 %collective-permute-start.5 = (f32[6,64,512]{2,1,0:T(8,128)}, f32[6,64,512]{2,1,0:T(8,128)S(1)}, u32[]{:S(2)}, u32[]{:S(2)}) collective-permute-start(f32[6,64,512]{2,1,0:T(8,128)} %get-tuple-element.10), channel_id=1, source_target_pairs={{0,2},{1,3},{2,4},{3,5},{4,6},{5,7},{6,0},{7,1},{8,10},{9,11},{10,... | collective-permute-start | bytes 2359304 | tf_op jit(solution)/shard_map/ppermute | solution.py:61
  101.2 39.4 %collective-permute-start.6 = (f32[6,64,512]{2,1,0:T(8,128)}, f32[6,64,512]{2,1,0:T(8,128)S(1)}, u32[]{:S(2)}, u32[]{:S(2)}) collective-permute-start(f32[6,64,512]{2,1,0:T(8,128)} %get-tuple-element.9), channel_id=1, source_target_pairs={{0,1},{1,2},{2,3},{3,4},{4,5},{5,6},{6,7},{7,0},{8,9},{9,10},{10,1... | collective-permute-start | bytes 2359304 | tf_op jit(solution)/shard_map/ppermute | solution.py:61
  160.0 12.3 %copy-start.4 = (f32[256]{0:T(256)S(1)}, f32[256]{0:T(256)}, u32[]{:S(2)}) copy-start(f32[256]{0:T(256)} %param.7) | copy-start | bytes 3076
  160.0 15.8 %copy-start.5 = (f32[512]{0:T(512)S(1)}, f32[512]{0:T(512)}, u32[]{:S(2)}) copy-start(f32[512]{0:T(512)} %param.8) | copy-start | bytes 6148
  160.0 102.8 %all-to-all-start.1 = ((f32[32,64,512]{2,1,0:T(8,128)}), f32[32,64,512]{2,1,0:T(8,128)}, u32[]{:S(2)}, u32[]{:S(2)}) async-start(f32[32,64,512]{2,1,0:T(8,128)} %shard_map.56), calls=%async_computation.1 | async-start | bytes 8388608 | tf_op jit(solution)/shard_map/all_to_all | solution.py:65
  262.8 10.6 %copy-start.2 = (f32[2048,512]{1,0:T(8,128)S(1)}, f32[2048,512]{1,0:T(8,128)}, u32[]{:S(2)}) copy-start(f32[2048,512]{1,0:T(8,128)} %fusion.20) | copy-start | bytes 12582916
  377.3 4.4 %copy-start.1 = (f32[768,512]{1,0:T(8,128)S(1)}, f32[768,512]{1,0:T(8,128)}, u32[]{:S(2)}) copy-start(f32[768,512]{1,0:T(8,128)} %param.6) | copy-start | bytes 4718596

commit v2 on v1

v2 whole, which is shorter than its diff:
```python
import functools

import jax
import jax.numpy as jnp
from jax import lax
from jax.experimental import pallas as pl
from jax.experimental.pallas import tpu as pltpu
from jax.sharding import PartitionSpec as P

MESH = pl.DeviceIdType.MESH
CAPACITY = 6
NZ, NX, NY, NC = 8, 4, 4, 2
GROUPS = NY * NC
PIECE = 64
ROWS = PIECE * NX
WIDTH = 512
PANEL = 128
PANELS = WIDTH // PANEL
PANEL_AT = [sum(WIDTH - PANEL * k for k in range(j)) for j in range(PANELS)]
PACKED = sum(WIDTH - PANEL * k for k in range(PANELS))
OWN, PAR, OUT = 0, 1, 2
F32, BF16 = jnp.float32, jnp.bfloat16


def split(x):
    high = x.astype(BF16)
    return high, (x - high.astype(F32)).astype(BF16)


def dot3(ah, al, bh, bl):
    d = functools.partial(jnp.dot, preferred_element_type=F32)
    return d(ah, bh) + (d(ah, bl) + d(al, bh))


def kernel(
    chosen_ref, place_ref, energy_ref, rows_ref, ve_row_ref, ve_col_ref, out_ref,
    mine, outbound, inbound, own, par, raw, ps, rs, pc, rc, dense, leaf,
    th, tl, rh, rl, fh, fl,
    xs, xr, os, orr, zs, zr, ls,
):
    aux = lax.axis_index("aux")
    occ = lax.axis_index("occ")
    z = aux // NX
    x = lax.rem(aux, NX)
    core = lax.rem(occ, NC)
    sign = 1 - 2 * core
    down = lax.rem(z - sign + NZ, NZ) * NX + x
    up = lax.rem(z + sign + NZ, NZ) * NX + x

    def to_aux(d):
        return {"aux": d, "occ": occ}

    def x_peer(dx):
        return z * NX + lax.rem(x + dx, NX)

    load = pltpu.make_async_copy(rows_ref, mine, ls.at[0])
    load.start()

    barrier = pltpu.get_barrier_semaphore()
    for d in (down, up, x_peer(1), x_peer(2), x_peer(3)):
        pl.semaphore_signal(barrier, inc=1, device_id=to_aux(d), device_id_type=MESH)
    for d in range(1, GROUPS):
        pl.semaphore_signal(
            barrier, inc=1, device_id={"aux": aux, "occ": lax.rem(occ + d, GROUPS)}, device_id_type=MESH
        )
    pl.semaphore_wait(barrier, 5 + GROUPS - 1)
    load.wait()

    def owner_z(n):
        half, odd = n // 2, lax.rem(n, 2)
        r = (1 - odd) * (half - 4) + odd * (3 - half)
        return lax.rem(z + sign * r + NZ, NZ)

    my_rows = pl.ds(pl.multiple_of(x * PIECE, PIECE), PIECE)

    def x_copies(kind, n):
        zo = owner_z(n)
        made = []
        for dx in range(NX):
            xd = lax.rem(x + dx, NX)
            if kind == OUT:
                src = dense.at[n, pl.ds(pl.multiple_of(xd * PIECE, PIECE), PIECE)]
                dst = out_ref.at[zo * NX + x]
            else:
                src = mine.at[zo * NX + xd]
                dst = (own, par)[kind].at[n, my_rows]
            if dx == 0:
                made.append(pltpu.make_async_copy(src, dst, xs.at[kind, n, 0]))
            else:
                made.append(
                    pltpu.make_async_remote_copy(
                        src_ref=src, dst_ref=dst, send_sem=xs.at[kind, n, dx], recv_sem=xr.at[kind, n, dx],
                        device_id=to_aux(x_peer(dx)), device_id_type=MESH,
                    )
                )
        return made

    def x_start(kind, n):
        for c in x_copies(kind, n):
            c.start()

    def x_arrived(kind, n):
        c = x_copies(kind, n)
        c[0].wait()
        for dx in range(1, NX):
            c[dx].wait_recv()

    def x_sent(kind, n):
        for c in x_copies(kind, n)[1:]:
            c.wait_send()

    def occ_copy(d):
        return pltpu.make_async_remote_copy(
            src_ref=outbound.at[d - 1], dst_ref=inbound.at[GROUPS - d],
            send_sem=os.at[d], recv_sem=orr.at[d],
            device_id={"aux": aux, "occ": lax.rem(occ + d, GROUPS)}, device_id_type=MESH,
        )

    def z_copy(kind, t):
        rows = (own, par)[kind]
        p, r = ((ps, rs), (pc, rc))[kind]
        src, dst, d = {
            0: (rows.at[0], raw.at[kind, 0], down),
            1: (rows.at[1], raw.at[kind, 1], up),
            2: (p.at[0], r.at[0], down),
            3: (p.at[1], r.at[1], up),
            4: (p.at[2], r.at[2], down),
            5: (p.at[3], r.at[3], up),
            6: (p.at[4], r.at[4], down),
            7: (p.at[5], r.at[2], up),
            8: (p.at[5], r.at[1], down),
            9: (r.at[2], r.at[0], up),
            10: (r.at[1], r.at[6], down),
            11: (r.at[0], r.at[5], up),
            12: (leaf.at[0], dense.at[0], up),
            13: (leaf.at[1], dense.at[1], down),
        }[t]
        return pltpu.make_async_remote_copy(
            src_ref=src, dst_ref=dst, send_sem=zs.at[kind, t], recv_sem=zr.at[kind, t],
            device_id=to_aux(d), device_id_type=MESH,
        )

    def send(kind, t):
        z_copy(kind, t).start()

    def arrived(kind, t):
        z_copy(kind, t).wait_recv()

    def products(kind, a, b, dst, add):
        rh[...], rl[...] = split(a[...])
        th[...], tl[...] = split(b[...].T)
        if kind == OWN:
            for j in range(PANELS):
                at, cols = PANEL * j, slice(PANEL * j, PANEL * (j + 1))
                v = dot3(th[at:, :], tl[at:, :], rh[:, cols], rl[:, cols])
                rows = slice(PANEL_AT[j], PANEL_AT[j] + WIDTH - at)
                dst[rows, :] = dst[rows, :] + v if add else v
        else:

            @pl.loop(0, 2)
            def _(h):
                rows = pl.ds(pl.multiple_of(h * 256, 256), 256)
                v = dot3(th[rows, :], tl[rows, :], rh[...], rl[...])
                dst[rows, :] = dst[rows, :] + v if add else v

    def partial_products(kind, n):
        x_arrived(kind, n)
        if kind == OWN:
            products(OWN, own.at[n], own.at[n], ps.at[n - 2], False)
        else:
            products(PAR, own.at[n], par.at[n], pc.at[n - 2], False)

    def accumulate(kind, p, r):
        dst, src = ((ps, rs), (pc, rc))[kind]
        dst[p] = dst[p] + src[r]

    def to_amplitude(kind):
        if kind == OWN:
            for j in range(PANELS):
                at = PANEL * j
                rows = slice(PANEL_AT[j], PANEL_AT[j] + WIDTH - at)
                pair = ve_col_ref[at:, :] + ve_row_ref[0:1, at : at + PANEL] - energy_ref[0]
                ps[5, rows, :] = (ps[5, rows, :] + rs[3, rows, :] + rs[4, rows, :]) / pair
        else:
            for j in range(PANELS):
                cols = slice(PANEL * j, PANEL * (j + 1))
                pair = ve_col_ref[...] + ve_row_ref[0:1, cols] - energy_ref[1]
                pc[5, :, cols] = (pc[5, :, cols] + rc[3, :, cols] + rc[4, :, cols]) / pair

    def unpack(kind, p):
        own_t, other_t = ((ps, rs), (pc, rc))[kind]
        t = own_t.at[5] if p == 5 else other_t.at[(5, 6, 0, 1, 2)[p]]
        if kind == OWN:
            for j in range(PANELS):
                at = PANEL * j
                cols = slice(at, at + PANEL)
                v = t[PANEL_AT[j] : PANEL_AT[j] + WIDTH - at, :]
                fh[at:, cols], fl[at:, cols] = split(v)
                for i in range(j + 1, PANELS):
                    over = slice(PANEL * i, PANEL * (i + 1))
                    w = v[PANEL * (i - j) : PANEL * (i - j + 1), :].T
                    fh[cols, over], fl[cols, over] = split(w)
        else:
            fh[...], fl[...] = split(t[...])

    def apply(kind, src, dst):
        rh[...], rl[...] = split(src[...])

        @pl.loop(0, 2)
        def _(h):
            cols = pl.ds(pl.multiple_of(h * 256, 256), 256)
            v = dot3(rh[...], rl[...], fh[:, cols], fl[:, cols])
            dst[:, cols] = v if kind == OWN else dst[:, cols] + v

    def density(kind, p):
        unpack(kind, p)
        apply(kind, (own, par)[kind].at[p + 2], dense.at[p + 2])

    def density_leaf(kind, p):
        unpack(kind, p)
        apply(kind, raw.at[kind, p], leaf.at[p])
        if kind == PAR:
            send(kind, 12 + p)
        apply(kind, (own, par)[kind].at[p + 2], dense.at[p + 2])

    @pl.loop(0, NZ)
    def _(n):
        x_start(OWN, n)

    for d in range(1, GROUPS):

        @pl.loop(0, CAPACITY)
        def _(s):
            outbound[d - 1, s] = mine[chosen_ref[d, s]]

        occ_copy(d).start()

    @pl.loop(0, CAPACITY)
    def _(s):
        inbound[0, s] = mine[chosen_ref[0, s]]

    def inward(kind, between):
        for n in range(2):
            x_arrived(kind, n)
            send(kind, n)
        for n in (2, 3):
            partial_products(kind, n)
        between(0)
        a = raw.at[OWN]
        b = raw.at[kind]
        p = (ps, pc)[kind]
        for j in range(2):
            arrived(kind, j)
            products(kind, a.at[j], b.at[j], p.at[j], True)
            send(kind, 2 + j)
        for n in (4, 5):
            partial_products(kind, n)
        between(1)
        for j in range(2):
            arrived(kind, 2 + j)
            accumulate(kind, 2 + j, j)
            send(kind, 4 + j)
        for n in (6, 7):
            partial_products(kind, n)
        between(2)
        arrived(kind, 4)
        accumulate(kind, 4, 2)
        send(kind, 6)
        between(3)
        arrived(kind, 5)
        arrived(kind, 6)
        to_amplitude(kind)
        send(kind, 7)
        send(kind, 8)

    inward(OWN, lambda k: None)

    @pl.loop(0, NZ)
    def _(n):
        x_sent(OWN, n)

    for d in range(1, GROUPS):
        occ_copy(d).wait_recv()

    @pl.loop(0, NZ)
    def _(n):
        zo = owner_z(n)
        for k in range(NX):
            at = place_ref[zo * NX + k]
            mine[zo * NX + k] = inbound[at // CAPACITY, lax.rem(at, CAPACITY)]
        x_start(PAR, n)

    arrived(OWN, 7)
    send(OWN, 9)
    arrived(OWN, 8)
    send(OWN, 10)
    arrived(OWN, 9)
    send(OWN, 11)

    def between(k):
        if k == 0:
            density(OWN, 5)
            density(OWN, 4)
            density(OWN, 3)
        if k == 1:
            arrived(OWN, 10)
            density_leaf(OWN, 1)
            density(OWN, 2)
        if k == 2:
            arrived(OWN, 11)
            density_leaf(OWN, 0)

    inward(PAR, between)

    arrived(PAR, 7)
    send(PAR, 9)
    arrived(PAR, 8)
    send(PAR, 10)
    density(PAR, 5)
    x_start(OUT, 7)
    arrived(PAR, 9)
    send(PAR, 11)
    density(PAR, 4)
    x_start(OUT, 6)
    density(PAR, 3)
    x_start(OUT, 5)
    arrived(PAR, 10)
    density_leaf(PAR, 1)
    x_start(OUT, 3)
    density(PAR, 2)
    x_start(OUT, 4)
    arrived(PAR, 11)
    density_leaf(PAR, 0)
    x_start(OUT, 2)
    for n in range(2):
        arrived(PAR, 12 + n)
        x_start(OUT, n)

    for kind in (OWN, PAR):
        for t in range(14 if kind == PAR else 12):
            z_copy(kind, t).wait_send()
    for d in range(1, GROUPS):
        occ_copy(d).wait_send()

    @pl.loop(0, NZ)
    def _(n):
        x_sent(PAR, n)
        x_arrived(OUT, n)
        x_sent(OUT, n)


def local(half_integrals, virtual_orbitals, occupied_energy, virtual_energy, partners):
    groups = lax.axis_size("occ")
    me = lax.axis_index("occ")
    column = lax.axis_index("aux")
    slices, size, _ = half_integrals.shape
    width = virtual_orbitals.shape[1]
    table = partners.reshape(groups, size)
    source = table // size
    index = table % size
    ids = jnp.arange(size, dtype=jnp.int32)
    same = source[:, :, None] == source[:, None, :]
    rank = jnp.sum((same & (ids[:, None] > ids[None, :])[None]).astype(jnp.int32), axis=2)
    slots = jnp.arange(CAPACITY, dtype=jnp.int32)
    match = (source == me)[:, None, :] & (rank[:, None, :] == slots[None, :, None])
    chosen = jnp.sum(jnp.where(match, index[:, None, :], 0), axis=2)
    turned = lax.rem(me + jnp.arange(groups, dtype=jnp.int32), groups)
    turn = turned[:, None] == jnp.arange(groups, dtype=jnp.int32)[None, :]
    chosen = jnp.sum(jnp.where(turn[:, :, None], chosen[None], 0), axis=1)
    my_source = lax.dynamic_index_in_dim(source, me, 0, keepdims=False)
    my_rank = lax.dynamic_index_in_dim(rank, me, 0, keepdims=False)
    my_place = lax.rem(my_source - me + groups, groups) * CAPACITY + my_rank

    first = me * size + column
    orbital_ids = jnp.arange(groups * size, dtype=jnp.int32)
    pick = lambda i: jnp.sum(jnp.where(orbital_ids == i, occupied_energy, jnp.float32(0.0)))
    own_energy = pick(first)
    partner_energy = pick(jnp.sum(jnp.where(orbital_ids == first, partners[:, 0], 0)))
    energy = jnp.stack([own_energy + own_energy, own_energy + partner_energy])

    rows = jnp.einsum(
        "qim,mv->iqv", half_integrals, virtual_orbitals, precision=lax.Precision.HIGHEST
    )
    vmem = lambda *s: pltpu.VMEM(s, F32)
    dma = pltpu.SemaphoreType.DMA
    smem = pl.BlockSpec(memory_space=pltpu.SMEM)
    out = pl.pallas_call(
        kernel,
        out_shape=jax.ShapeDtypeStruct((size, slices, width), F32),
        in_specs=[smem, smem, smem, pl.BlockSpec(memory_space=pl.ANY)]
        + [pl.BlockSpec(memory_space=pltpu.VMEM)] * 2,
        out_specs=pl.BlockSpec(memory_space=pl.ANY),
        scratch_shapes=[
            vmem(size, slices, width),
            vmem(GROUPS - 1, CAPACITY, slices, width),
            vmem(GROUPS, CAPACITY, slices, width),
            vmem(NZ, ROWS, WIDTH),
            vmem(NZ, ROWS, WIDTH),
            vmem(2, 2, ROWS, WIDTH),
            vmem(6, PACKED, PANEL),
            vmem(7, PACKED, PANEL),
            vmem(6, WIDTH, WIDTH),
            vmem(7, WIDTH, WIDTH),
            vmem(NZ, ROWS, WIDTH),
            vmem(2, ROWS, WIDTH),
            pltpu.VMEM((WIDTH, ROWS), BF16),
            pltpu.VMEM((WIDTH, ROWS), BF16),
            pltpu.VMEM((ROWS, WIDTH), BF16),
            pltpu.VMEM((ROWS, WIDTH), BF16),
            pltpu.VMEM((WIDTH, WIDTH), BF16),
            pltpu.VMEM((WIDTH, WIDTH), BF16),
            dma((3, NZ, NX)),
            dma((3, NZ, NX)),
            dma((GROUPS,)),
            dma((GROUPS,)),
            dma((2, 14)),
            dma((2, 14)),
            dma((1,)),
        ],
        compiler_params=pltpu.CompilerParams(
            collective_id=0, has_side_effects=True, vmem_limit_bytes=62 * 1024 * 1024
        ),
    )(
        chosen,
        my_place,
        energy,
        rows,
        virtual_energy[None, :],
        jnp.broadcast_to(virtual_energy[:, None], (width, PANEL)),
    )
    return jnp.transpose(out, (1, 0, 2))


def solution(mesh):
    return jax.shard_map(
        local,
        mesh=mesh,
        in_specs=(P("aux", "occ", None), P(), P(), P(), P()),
        out_specs=P("aux", "occ", None),
        check_vma=False,
    )
```

time: 387 us -> 315 us (0.81)
  Pallas kernels: 45.2 us -> 278 us
  waiting for transfers between devices: 129 us -> 0 us
  blocking collectives: 98.6 us -> 0 us
  matrix products: 49.3 us -> 16.8 us
  starting transfers between devices: 30.7 us -> 0 us
  local copies, waits for them, and re-layouts: 22.9 us -> 9.4 us
    pallas_call x2 -> x1, Pallas kernels: 45.2 us -> 278 us  [local(): pl.pallas_call(kernel, out_shape=jax.ShapeDtypeStruct((size, slices, widt...]
    all_to_all x1 -> x0, blocking collectives: 98.6 us -> none  [local(): lax.all_to_all(density.reshape(columns, slices, width), 'aux', split_axis...]
    all_to_all x2 -> x0, waiting for transfers between devices: 69.4 us -> none  [the longest x1 69.4 us: local(): lax.all_to_all(partner_rows, 'aux', split_axis=0, concat_axis=0, tiled=True)]
    ppermute x7 -> x0, waiting for transfers between devices: 59.6 us -> none  [local(): lax.ppermute(outbound[d], 'occ', [(g, (g + d) % groups) for g in range(gr...]
    dot_general x5 -> x1, matrix products: 49.3 us -> 16.8 us  [local(): jnp.einsum('qim,mv->iqv', half_integrals, virtual_orbitals, precision=lax...]
    all_to_all x2 -> x0, starting transfers between devices: 23.4 us -> none  [the longest x1 11.8 us: local(): own = lax.all_to_all(rows, 'aux', split_axis=0, concat_axis=0, tiled=True)]
    unnamed x20 -> x3, local copies, waits for them, and re-layouts: 11.1 us -> 0.51 us
    ppermute x7 -> x0, starting transfers between devices: 7.24 us -> none  [local(): lax.ppermute(outbound[d], 'occ', [(g, (g + d) % groups) for g in range(gr...]
  transfers between devices with their start and end apart: 9 -> 0, of which waited for: 6 -> 0; matrix products, arithmetic and copies ran while one was open for 10% -> 0% of each run, Pallas kernels for 12% -> 0%
where the time goes in v2:
time: 315 us; the launch traced here: 313 us
  Pallas kernels  278 us (88%)
  matrix products  16.8 us (5%)
  local copies, waits for them, and re-layouts  9.4 us (3%)
  other arithmetic  6.73 us (2%)
    pallas_call x1, Pallas kernels, local(): pl.pallas_call(kernel, out_shape=jax.ShapeDtypeStruct((size, slices, widt...  278 us
    dot_general x1, matrix products, local(): jnp.einsum('qim,mv->iqv', half_integrals, virtual_orbitals, precision=lax...  16.8 us
    transpose x1, local copies, waits for them, and re-layouts, local(): return jnp.transpose(out, (1, 0, 2))  6.63 us

profile of v2, /device:TPU:2, one launch (start us, length us, event | category | flops | bytes accessed | tf_op | source)
XLA Modules:
  0.0 313.1 jit_solution(8872073440136382248)
XLA Ops:
  0.0 0.0 copy-start
  0.0 1.4 select_reduce_fusion.2
  1.4 2.0 fusion.9
  5.9 0.7 pad_maximum_fusion.energy_ref
  6.5 0.5 broadcast.164
  7.0 1.3 reduce.3
  8.4 0.1 iota_compare_fusion.2
  8.5 0.1 reshape.139
  8.6 0.3 convert_reduce_fusion
  8.9 0.6 fusion.13.place_ref
  9.5 0.2 select_reduce_fusion.1
  9.6 0.2 select_reduce_fusion
  9.8 0.7 copy.9.chosen_ref
  10.5 1.5 broadcast_in_dim.71.ve_col_ref
  12.0 0.0 copy-done
  12.0 16.8 %fusion.2.rows_ref = f32[32,64,512]{2,1,0:T(8,128)} fusion(f32[64,32,768]{2,1,0:T(8,128)} %param.5, f32[768,512]{1,0:T(8,128)S(1)} %copy-done), kind=kOutput, calls=%fused_computation.2 | convolution fusion | flops 9663676416 | bytes 12058624 | tf_op jit(solution)/shard_map/qim,mv->iqv/dot_general | solution.py:381
  28.8 277.7 %shard_map.55 = f32[32,64,512]{2,1,0:T(8,128)} custom-call(s32[8,6]{1,0:T(8,128)} %copy.9.chosen_ref, s32[32]{0:T(128)} %fusion.13.place_ref, f32[2]{0:T(128)} %pad_maximum_fusion.energy_ref, f32[32,64,512]{2,1,0:T(8,128)} %fusion.2.rows_ref, f32[1,512]{1,0:T(1,128)} %bitcast.16, f32[512,128]{1,0:T(8,128)} %broadcast_in_dim.71.ve_col_ref), custom_call_target="tpu_custom_call" | custom-call | tf_op jit(solution)/shard_map/pallas_call | solution.py:387
  306.5 6.6 %copy.10 = f32[64,32,512]{2,1,0:T(8,128)} copy(f32[64,32,512]{2,0,1:T(8,128)} %bitcast.15) | data formatting | bytes 8388608 | tf_op jit(solution)/shard_map/transpose | solution.py:431
  (4 shorter events, 0.0 us)
Async XLA Ops:
  0.0 12.0 %copy-start = (f32[768,512]{1,0:T(8,128)S(1)}, f32[768,512]{1,0:T(8,128)}, u32[]{:S(2)}) copy-start(f32[768,512]{1,0:T(8,128)} %param.6) | copy-start | bytes 4718596

commit v3 on v2

v3 whole, which is shorter than its diff:
```python
import functools

import jax
import jax.numpy as jnp
from jax import lax
from jax.experimental import pallas as pl
from jax.experimental.pallas import tpu as pltpu
from jax.sharding import PartitionSpec as P

MESH = pl.DeviceIdType.MESH
CAPACITY = 6
NZ, NX, NY, NC = 8, 4, 4, 2
GROUPS = NY * NC
PIECE = 64
GO, SUB = 32, 8
ROWS = PIECE * NX
WIDTH = 512
PANEL = 128
PANELS = WIDTH // PANEL
OFF = [(j, i) for j in range(PANELS) for i in range(j + 1, PANELS)]
SPARE = PANEL * (len(OFF) + PANELS // 2)
PACKED = SPARE + 8
CUTS = ((0, PACKED // 16 * 8, PACKED), (0, WIDTH // 2, WIDTH))
OWN, PAR, OUT = 0, 1, 2
PARTS = 2
F32, BF16 = jnp.float32, jnp.bfloat16


def split(x):
    high = x.astype(BF16)
    return high, (x - high.astype(F32)).astype(BF16)


def dot3(ah, al, bh, bl):
    d = functools.partial(jnp.dot, preferred_element_type=F32)
    return d(ah, bh) + (d(ah, bl) + d(al, bh))


def kernel(
    partners_ref, occupied_ref, partner_row_ref, partner_col_ref, half_ref, orbitals_ref, ve_row_ref, out_ref,
    mine, pool, inbound, own, par, raw, ps, rs, pc, rc,
    th, tl, rh, rl, fh, fl, half, wh, wl, ah, al, vc, table_v, place_v, table_s, place_s,
    xs, xr, os, orr, zs, zr, ls,
):
    aux = lax.axis_index("aux")
    occ = lax.axis_index("occ")
    z = aux // NX
    x = lax.rem(aux, NX)
    core = lax.rem(occ, NC)
    sign = 1 - 2 * core
    z_down = lax.rem(z - sign + NZ, NZ) * NX
    z_up = lax.rem(z + sign + NZ, NZ) * NX
    down, up = z_down + x, z_up + x

    def to_aux(d):
        return {"aux": d, "occ": occ}

    def x_turn(dx):
        return lax.rem(x + dx, NX)

    loads = [
        pltpu.make_async_copy(
            half_ref.at[:, pl.ds(SUB * c, SUB), pl.ds(PANEL * m, PANEL)], half.at[c, m], ls.at[c, m]
        )
        for c in range(half.shape[0])
        for m in range(half.shape[1])
    ]
    for c in loads:
        c.start()

    barrier = pltpu.get_barrier_semaphore()
    near = [z_down + x_turn(k) for k in range(NX)] + [z_up + x_turn(k) for k in range(NX)]
    near += [z * NX + x_turn(k) for k in range(1, NX)]
    for d in near:
        pl.semaphore_signal(barrier, inc=1, device_id=to_aux(d), device_id_type=MESH)
    for d in range(1, GROUPS):
        pl.semaphore_signal(
            barrier, inc=1, device_id={"aux": aux, "occ": lax.rem(occ + d, GROUPS)}, device_id_type=MESH
        )

    wh[...], wl[...] = split(orbitals_ref[...])
    total = GROUPS * GO
    row, col = partner_row_ref[...], partner_col_ref[...]
    shift = lambda v: lax.shift_right_logical(v, jnp.full_like(v, 5))
    lane = lax.broadcasted_iota(jnp.int32, (total, total), 1)
    sub = lax.broadcasted_iota(jnp.int32, (total, total), 0)
    ahead = (shift(col) == shift(row)) & (shift(lane) == shift(sub)) & (sub < lane)
    rank = jnp.sum(jnp.where(ahead, 1, 0), axis=0, keepdims=True)
    source = shift(row)
    place = ((source - occ) & (GROUPS - 1)) * CAPACITY + jnp.minimum(rank, CAPACITY - 1)
    place_v[...] = jnp.broadcast_to(place, (8, total))
    asker = shift(lax.broadcasted_iota(jnp.int32, (GROUPS, total), 1))
    turned = (occ + lax.broadcasted_iota(jnp.int32, (GROUPS, total), 0)) & (GROUPS - 1)
    slot = lax.broadcasted_iota(jnp.int32, (GROUPS, PANEL), 1)
    table = jnp.zeros((GROUPS, PANEL), jnp.int32)
    for s in range(CAPACITY):
        pick = jnp.where((source == occ) & (rank == s), row & (GO - 1), 0)
        found = jnp.sum(jnp.where(asker == turned, pick, 0), axis=1, keepdims=True)
        table = jnp.where(slot == s, found, table)
    table_v[...] = table
    to_table = pltpu.make_async_copy(table_v, table_s, ls.at[4, 0])
    to_place = pltpu.make_async_copy(place_v, place_s, ls.at[4, 1])
    to_table.start()
    to_place.start()
    vc[...] = jnp.broadcast_to(ve_row_ref[...], (PANEL, WIDTH)).T
    first = occ * GO + aux
    own_energy = occupied_ref[first]
    self_energy = own_energy + own_energy
    cross_energy = own_energy + occupied_ref[partners_ref[first]]
    pl.semaphore_wait(barrier, len(near) + GROUPS - 1)
    to_table.wait()
    to_place.wait()
    for c in loads:
        c.wait()

    def owner_z(n):
        half_n, odd = n // 2, lax.rem(n, 2)
        r = (1 - odd) * (half_n - 4) + odd * (3 - half_n)
        return lax.rem(z + sign * r + NZ, NZ)

    def block(ref, i, count=1):
        return ref.at[i] if count == 1 else ref.at[pl.ds(i, count)]

    def rows_of(ref, i):
        return ref.at[pl.ds(pl.multiple_of(i * PIECE, PIECE), PIECE)]

    def dense(n):
        return block(pool, (n - 2) * NX, NX)

    def leaf(j):
        return block(pool, (6 + j) * NX, NX)

    def remote(kind, n, dx, src, dst, d):
        return pltpu.make_async_remote_copy(
            src_ref=src, dst_ref=dst, send_sem=xs.at[kind, n, dx], recv_sem=xr.at[kind, n, dx],
            device_id=to_aux(d), device_id_type=MESH,
        )

    def end_copies(kind, n):
        made = []
        for dx in range(NX):
            xd = x_turn(dx)
            if kind == OUT:
                src = block(leaf(n), xd)
                dst = out_ref.at[owner_z(n + 2) * NX + x]
                d = (z_up, z_down)[n] + xd
            else:
                src = block(mine, owner_z(n) * NX + xd)
                dst = rows_of(raw.at[kind, n], x)
                d = (z_down, z_up)[n] + xd
            made.append(remote(kind, n, dx, src, dst, d))
        return made

    def x_copies(kind, n):
        zo = owner_z(n)
        made = []
        for dx in range(NX):
            xd = x_turn(dx)
            if kind == OUT:
                src = block(pool, (n - 2) * NX + xd)
                dst = out_ref.at[zo * NX + x]
            else:
                src = block(mine, zo * NX + xd)
                dst = rows_of((own, par)[kind].at[n - 2], x)
            if dx == 0:
                made.append(pltpu.make_async_copy(src, dst, xs.at[kind, n, 0]))
            else:
                made.append(remote(kind, n, dx, src, dst, z * NX + xd))
        return made

    def start(copies):
        for c in copies:
            c.start()

    def x_arrived(kind, n):
        c = x_copies(kind, n)
        c[0].wait()
        for dx in range(1, NX):
            c[dx].wait_recv()

    def x_sent(kind, n):
        for c in x_copies(kind, n)[1:]:
            c.wait_send()

    def end_arrived(kind, n):
        for c in end_copies(kind, n):
            c.wait_recv()

    def end_sent(kind, n):
        for c in end_copies(kind, n):
            c.wait_send()

    def occ_copy(d):
        return pltpu.make_async_remote_copy(
            src_ref=block(pool, (d - 1) * CAPACITY, CAPACITY),
            dst_ref=block(inbound, (GROUPS - d) * CAPACITY, CAPACITY),
            send_sem=os.at[d], recv_sem=orr.at[d],
            device_id={"aux": aux, "occ": lax.rem(occ + d, GROUPS)}, device_id_type=MESH,
        )

    def part(kind, h):
        return pl.ds(CUTS[kind][h], CUTS[kind][h + 1] - CUTS[kind][h])

    def z_copy(kind, t, h):
        p, r = ((ps, rs), (pc, rc))[kind]
        src, dst, d = {
            2: (p.at[0], r.at[0], down),
            3: (p.at[1], r.at[1], up),
            4: (p.at[2], r.at[2], down),
            5: (p.at[3], r.at[3], up),
            6: (p.at[4], r.at[4], down),
            7: (p.at[5], r.at[2], up),
            8: (p.at[5], r.at[1], down),
            9: (r.at[2], r.at[0], up),
            10: (r.at[1], r.at[6], down),
            11: (r.at[0], r.at[5], up),
        }[t]
        rows = part(kind, h)
        return pltpu.make_async_remote_copy(
            src_ref=src.at[rows], dst_ref=dst.at[rows], send_sem=zs.at[kind, t, h], recv_sem=zr.at[kind, t, h],
            device_id=to_aux(d), device_id_type=MESH,
        )

    def send(kind, t, h):
        z_copy(kind, t, h).start()

    def arrived(kind, t, h):
        z_copy(kind, t, h).wait_recv()

    def pass_on(kind, t, then):
        for h in range(PARTS):
            arrived(kind, t, h)
            send(kind, then, h)

    def first_product(n):
        zo = owner_z(n)
        for m in range(half.shape[1]):
            at = half.at[zo // 2, m].reshape(PIECE * SUB, PANEL)
            cols = slice(PANEL * m, PANEL * (m + 1))
            for k in range(NX):
                rows = slice(PIECE * k, PIECE * (k + 1))
                v = at[pl.ds(lax.rem(zo, 2) * NX + k, PIECE, stride=SUB), :]
                ah[rows, cols], al[rows, cols] = split(v)

        @pl.loop(0, 2)
        def _(h):
            cols = pl.ds(pl.multiple_of(h * 256, 256), 256)
            v = dot3(ah[...], al[...], wh[:, cols], wl[:, cols])
            for k in range(NX):
                mine[zo * NX + k, :, cols] = v[PIECE * k : PIECE * (k + 1), :]

    tile_row = lax.broadcasted_iota(jnp.int32, (PANEL, PANEL), 0)
    tile_col = lax.broadcasted_iota(jnp.int32, (PANEL, PANEL), 1)
    low, diagonal = tile_row >= tile_col, tile_row == tile_col
    spare = lax.broadcasted_iota(jnp.int32, (8, PANEL), 0)

    def pair_block(i, j):
        return vc[PANEL * i : PANEL * (i + 1), :] + ve_row_ref[0:1, PANEL * j : PANEL * (j + 1)] - self_energy

    def products(kind, a, b, dst, add):
        rh[...], rl[...] = split(a[...])
        th[...], tl[...] = split(b[...].T)
        if kind == OWN:

            def put(at, v):
                rows = slice(at, at + v.shape[0])
                dst[rows, :] = dst[rows, :] + v if add else v

            extra = jnp.zeros((8, PANEL), F32)
            first = None
            for j in range(PANELS):
                at, cols = PANEL * j, slice(PANEL * j, PANEL * (j + 1))
                v = dot3(th[at:, :], tl[at:, :], rh[:, cols], rl[:, cols])
                if j + 1 < PANELS:
                    put(PANEL * OFF.index((j, j + 1)), v[PANEL:, :])
                if j % 2 == 0:
                    first = v[:PANEL, :]
                else:
                    second = v[:PANEL, :]
                    put(PANEL * (len(OFF) + j // 2), jnp.where(low, first, second))
                    d = jnp.sum(jnp.where(diagonal, second, 0.0), axis=0, keepdims=True)
                    extra = jnp.where(spare == j // 2, d, extra)
            put(SPARE, extra)
        else:

            @pl.loop(0, 2)
            def _(h):
                rows = pl.ds(pl.multiple_of(h * 256, 256), 256)
                v = dot3(th[rows, :], tl[rows, :], rh[...], rl[...])
                dst[rows, :] = dst[rows, :] + v if add else v

    def partial_products(kind, n):
        x_arrived(kind, n)
        if kind == OWN:
            products(OWN, own.at[n - 2], own.at[n - 2], ps.at[n - 2], False)
        else:
            products(PAR, own.at[n - 2], par.at[n - 2], pc.at[n - 2], False)

    def accumulate(kind, p, r, h):
        dst, src = ((ps, rs), (pc, rc))[kind]
        rows = part(kind, h)
        dst[p, rows, :] = dst[p, rows, :] + src[r, rows, :]

    def to_amplitude(kind, h):
        if kind == OWN:

            def divide(at, pair):
                rows = slice(at, at + pair.shape[0])
                ps[5, rows, :] = (ps[5, rows, :] + rs[3, rows, :] + rs[4, rows, :]) / pair

            for b, (j, i) in enumerate(OFF):
                if CUTS[OWN][h] <= PANEL * b < CUTS[OWN][h + 1]:
                    divide(PANEL * b, pair_block(i, j))
            if h == PARTS - 1:
                extra = jnp.ones((8, PANEL), F32)
                for k in range(PANELS // 2):
                    i, j = 2 * k, 2 * k + 1
                    divide(PANEL * (len(OFF) + k), jnp.where(low, pair_block(i, i), pair_block(j, j)))
                    ve = ve_row_ref[0:1, PANEL * j : PANEL * (j + 1)]
                    extra = jnp.where(spare == k, ve + ve - self_energy, extra)
                divide(SPARE, extra)
        else:
            rows = part(PAR, h)
            for j in range(PANELS):
                cols = slice(PANEL * j, PANEL * (j + 1))
                pair = vc[rows, :] + ve_row_ref[0:1, cols] - cross_energy
                pc[5, rows, cols] = (pc[5, rows, cols] + rc[3, rows, cols] + rc[4, rows, cols]) / pair

    def unpack(kind, p):
        own_t, other_t = ((ps, rs), (pc, rc))[kind]
        t = own_t.at[5] if p == 5 else other_t.at[(5, 6, 0, 1, 2)[p]]
        if kind == OWN:

            def put(i, j, v):
                at = slice(PANEL * i, PANEL * (i + 1)), slice(PANEL * j, PANEL * (j + 1))
                fh[at], fl[at] = split(v)

            for b, (j, i) in enumerate(OFF):
                v = t[PANEL * b : PANEL * (b + 1), :]
                put(i, j, v)
                put(j, i, v.T)
            for k in range(PANELS // 2):
                at = PANEL * (len(OFF) + k)
                v = t[at : at + PANEL, :]
                w = v.T
                put(2 * k, 2 * k, jnp.where(low, v, w))
                d = t[SPARE + k : SPARE + k + 1, :]
                put(2 * k + 1, 2 * k + 1, jnp.where(diagonal, d, jnp.where(low, w, v)))
        else:
            fh[...], fl[...] = split(t[...])

    def apply(kind, src, dst):
        rh[...], rl[...] = split(src[...])

        @pl.loop(0, 2)
        def _(h):
            cols = pl.ds(pl.multiple_of(h * 256, 256), 256)
            v = dot3(rh[...], rl[...], fh[:, cols], fl[:, cols])
            for k in range(NX):
                w = v[PIECE * k : PIECE * (k + 1), :]
                dst[k, :, cols] = w if kind == OWN else dst[k, :, cols] + w

    def density(kind, p):
        unpack(kind, p)
        apply(kind, (own, par)[kind].at[p], dense(p + 2))

    def density_leaf(kind, p):
        unpack(kind, p)
        apply(kind, raw.at[kind, p], leaf(p))
        if kind == PAR:
            start(end_copies(OUT, p))
        apply(kind, (own, par)[kind].at[p], dense(p + 2))

    def begin_occ():
        for d in range(1, GROUPS):

            @pl.loop(0, CAPACITY)
            def _(s):
                pool[(d - 1) * CAPACITY + s] = mine[table_s[d, s]]

            occ_copy(d).start()

        @pl.loop(0, CAPACITY)
        def _(s):
            inbound[s] = mine[table_s[0, s]]

    def inward(kind, between):
        p = (ps, pc)[kind]
        for j in range(2):
            partial_products(kind, 2 + j)
            end_arrived(kind, j)
            products(kind, raw.at[OWN, j], raw.at[kind, j], p.at[j], True)
            for h in range(PARTS):
                send(kind, 2 + j, h)
            between(j)
        for n in (4, 5):
            partial_products(kind, n)
        between(2)
        for j in range(2):
            for h in range(PARTS):
                arrived(kind, 2 + j, h)
                accumulate(kind, 2 + j, j, h)
                send(kind, 4 + j, h)
        for n in (6, 7):
            partial_products(kind, n)
        between(3)
        for h in range(PARTS):
            arrived(kind, 4, h)
            accumulate(kind, 4, 2, h)
            send(kind, 6, h)
        between(4)
        for h in range(PARTS):
            arrived(kind, 5, h)
            arrived(kind, 6, h)
            to_amplitude(kind, h)
            send(kind, 7, h)
            send(kind, 8, h)

    @pl.loop(0, 2)
    def _(j):
        @pl.loop(0, 2)
        def _(i):
            first_product(2 * i + j)

        for n in range(2):

            @pl.when(j == n)
            def _():
                start(end_copies(OWN, n))

        start(x_copies(OWN, 2 + j))

    @pl.loop(4, NZ)
    def _(n):
        first_product(n)

    begin_occ()

    def rest(k):
        if k < 2:
            start(x_copies(OWN, 4 + k))
            start(x_copies(OWN, 6 + k))

    inward(OWN, rest)

    pass_on(OWN, 7, 9)
    pass_on(OWN, 8, 10)

    for n in range(2):
        end_sent(OWN, n)

    @pl.loop(2, NZ)
    def _(n):
        x_sent(OWN, n)

    for d in range(1, GROUPS):
        occ_copy(d).wait_recv()
        occ_copy(d).wait_send()

    def take_partners(n):
        zo = owner_z(n)
        for k in range(NX):
            mine[zo * NX + k] = inbound[place_s[0, occ * GO + zo * NX + k]]

    for n in range(2):
        take_partners(n)
        start(end_copies(PAR, n))
        take_partners(n + 2)
        start(x_copies(PAR, n + 2))

    pass_on(OWN, 9, 11)

    @pl.loop(4, NZ)
    def _(n):
        take_partners(n)

    def between(k):
        if k < 2:
            start(x_copies(PAR, 4 + k))
            start(x_copies(PAR, 6 + k))
        if k == 0:
            density(OWN, 5)
        if k == 2:
            density(OWN, 4)
            density(OWN, 3)
        if k == 3:
            for h in range(PARTS):
                arrived(OWN, 10, h)
            density_leaf(OWN, 1)
            density(OWN, 2)
        if k == 4:
            for h in range(PARTS):
                arrived(OWN, 11, h)
            density_leaf(OWN, 0)

    inward(PAR, between)

    pass_on(PAR, 7, 9)
    pass_on(PAR, 8, 10)
    density(PAR, 5)
    start(x_copies(OUT, 7))
    pass_on(PAR, 9, 11)
    density(PAR, 4)
    start(x_copies(OUT, 6))
    density(PAR, 3)
    start(x_copies(OUT, 5))
    for h in range(PARTS):
        arrived(PAR, 10, h)
    density_leaf(PAR, 1)
    start(x_copies(OUT, 3))
    density(PAR, 2)
    start(x_copies(OUT, 4))
    for h in range(PARTS):
        arrived(PAR, 11, h)
    density_leaf(PAR, 0)
    start(x_copies(OUT, 2))

    for kind in (OWN, PAR):
        for t in range(2, 12):
            for h in range(PARTS):
                z_copy(kind, t, h).wait_send()

    for n in range(2):
        end_sent(PAR, n)
        end_arrived(OUT, n)
        end_sent(OUT, n)

    @pl.loop(2, NZ)
    def _(n):
        x_sent(PAR, n)
        x_arrived(OUT, n)
        x_sent(OUT, n)


def local(half_integrals, virtual_orbitals, occupied_energy, virtual_energy, partners):
    slices, size, atoms = half_integrals.shape
    width = virtual_orbitals.shape[1]
    total = partners.shape[0]
    vmem = lambda *s: pltpu.VMEM(s, F32)
    half_vmem = lambda *s: pltpu.VMEM(s, BF16)
    dma = pltpu.SemaphoreType.DMA
    smem = pl.BlockSpec(memory_space=pltpu.SMEM)
    whole = pl.BlockSpec(memory_space=pltpu.VMEM)
    hbm = pl.BlockSpec(memory_space=pl.ANY)
    flat = partners.reshape(total)
    out = pl.pallas_call(
        kernel,
        out_shape=jax.ShapeDtypeStruct((size, slices, width), F32),
        in_specs=[smem, smem, whole, whole, hbm, whole, whole],
        out_specs=hbm,
        scratch_shapes=[
            vmem(size, slices, width),
            vmem((GROUPS - 1) * CAPACITY, slices, width),
            vmem(GROUPS * CAPACITY, slices, width),
            vmem(NZ - 2, ROWS, WIDTH),
            vmem(NZ - 2, ROWS, WIDTH),
            vmem(2, 2, ROWS, WIDTH),
            vmem(6, PACKED, PANEL),
            vmem(7, PACKED, PANEL),
            vmem(6, WIDTH, WIDTH),
            vmem(7, WIDTH, WIDTH),
            half_vmem(WIDTH, ROWS),
            half_vmem(WIDTH, ROWS),
            half_vmem(ROWS, WIDTH),
            half_vmem(ROWS, WIDTH),
            half_vmem(WIDTH, WIDTH),
            half_vmem(WIDTH, WIDTH),
            vmem(size // SUB, atoms // PANEL, slices, SUB, PANEL),
            half_vmem(atoms, width),
            half_vmem(atoms, width),
            half_vmem(ROWS, atoms),
            half_vmem(ROWS, atoms),
            vmem(WIDTH, PANEL),
            pltpu.VMEM((GROUPS, PANEL), jnp.int32),
            pltpu.VMEM((8, total), jnp.int32),
            pltpu.SMEM((GROUPS, PANEL), jnp.int32),
            pltpu.SMEM((8, total), jnp.int32),
            dma((3, NZ, NX)),
            dma((3, NZ, NX)),
            dma((GROUPS,)),
            dma((GROUPS,)),
            dma((2, 12, PARTS)),
            dma((2, 12, PARTS)),
            dma((size // SUB + 1, atoms // PANEL)),
        ],
        compiler_params=pltpu.CompilerParams(
            collective_id=0, has_side_effects=True, vmem_limit_bytes=62 * 1024 * 1024
        ),
    )(
        flat,
        occupied_energy,
        flat[None, :],
        partners,
        half_integrals,
        virtual_orbitals,
        virtual_energy[None, :],
    )
    return jnp.transpose(out, (1, 0, 2))


def solution(mesh):
    return jax.shard_map(
        local,
        mesh=mesh,
        in_specs=(P("aux", "occ", None), P(), P(), P(), P()),
        out_specs=P("aux", "occ", None),
        check_vma=False,
    )
```

time: 315 us -> 270 us (0.86)
  Pallas kernels: 278 us -> 260 us
  matrix products: 16.8 us -> 0 us
  other arithmetic: 6.73 us -> 0 us
    pallas_call x1, Pallas kernels: 278 us -> 260 us  [local(): pl.pallas_call(kernel, out_shape=jax.ShapeDtypeStruct((size, slices, widt...]
    dot_general x1 -> x0, matrix products: 16.8 us -> none  [local(): jnp.einsum('qim,mv->iqv', half_integrals, virtual_orbitals, precision=lax...]
    reduce_sum x5 -> x0, other arithmetic: 4.04 us -> none  [the longest x1 1.96 us: local(): jnp.sum(jnp.where(orbital_ids == i, occupied_energy, jnp.float32(0.0)))]
where the time goes in v3:
time: 270 us; the launch traced here: 268 us
  Pallas kernels  260 us (96%)
  local copies, waits for them, and re-layouts  8.1 us (3%)
    pallas_call x1, Pallas kernels, local(): pl.pallas_call(kernel, out_shape=jax.ShapeDtypeStruct((size, slices, widt...  260 us
    transpose x1, local copies, waits for them, and re-layouts, local(): return jnp.transpose(out, (1, 0, 2))  6.63 us

profile of v3, /device:TPU:2, one launch (start us, length us, event | category | flops | bytes accessed | tf_op | source)
XLA Modules:
  0.0 268.3 jit_solution(7240801628790747465)
XLA Ops:
  0.0 1.5 copy.6.partner_col_ref
  1.5 260.2 %shard_map.55 = f32[32,64,512]{2,1,0:T(8,128)} custom-call(s32[256]{0:T(256)} %bitcast.5, f32[256]{0:T(256)} %occupied_ref.1, s32[1,256]{1,0:T(1,128)} %bitcast.6, s32[256,1]{1,0:T(8,128)} %copy.6.partner_col_ref, f32[64,32,768]{2,1,0:T(8,128)} %half_ref.1, f32[768,512]{1,0:T(8,128)} %orbitals_ref.1, f32[1,512]{1,0:T(1,128)} %bitcast.7), custom_call_target="tpu_custom_call" | custom-call | tf_op jit(solution)/shard_map/pallas_call | solution.py:546
  261.7 6.6 %copy.7 = f32[64,32,512]{2,1,0:T(8,128)} copy(f32[64,32,512]{2,0,1:T(8,128)} %bitcast.4) | data formatting | bytes 8388608 | tf_op jit(solution)/shard_map/transpose | solution.py:598

commit v4 on v3

--- a/solution.py
+++ b/solution.py
@@ -84,7 +84,15 @@
     shift = lambda v: lax.shift_right_logical(v, jnp.full_like(v, 5))
     lane = lax.broadcasted_iota(jnp.int32, (total, total), 1)
     sub = lax.broadcasted_iota(jnp.int32, (total, total), 0)
-    ahead = (shift(col) == shift(row)) & (shift(lane) == shift(sub)) & (sub < lane)
+
+
+    def use_order(request):
+        side = 1 - 2 * (shift(request) & (NC - 1))
+        away = (lax.shift_right_logical(request, jnp.full_like(request, 2)) & (NZ - 1)) - z
+        r = ((side * away + 4) & (NZ - 1)) - 4
+        return jnp.where(r < 0, 2 * (r + 4), 7 - 2 * r) * NX + (request & (NX - 1))
+
+    ahead = (shift(col) == shift(row)) & (shift(lane) == shift(sub)) & (use_order(sub) < use_order(lane))
     rank = jnp.sum(jnp.where(ahead, 1, 0), axis=0, keepdims=True)
     source = shift(row)
     place = ((source - occ) & (GROUPS - 1)) * CAPACITY + jnp.minimum(rank, CAPACITY - 1)
@@ -107,9 +115,6 @@
     own_energy = occupied_ref[first]
     self_energy = own_energy + own_energy
     cross_energy = own_energy + occupied_ref[partners_ref[first]]
-    pl.semaphore_wait(barrier, len(near) + GROUPS - 1)
-    to_table.wait()
-    to_place.wait()
     for c in loads:
         c.wait()
 
@@ -190,11 +195,12 @@
         for c in end_copies(kind, n):
             c.wait_send()
 
-    def occ_copy(d):
+    def occ_copy(d, h):
+        first_slot, count = ((0, NX), (NX, CAPACITY - NX))[h]
         return pltpu.make_async_remote_copy(
-            src_ref=block(pool, (d - 1) * CAPACITY, CAPACITY),
-            dst_ref=block(inbound, (GROUPS - d) * CAPACITY, CAPACITY),
-            send_sem=os.at[d], recv_sem=orr.at[d],
+            src_ref=block(pool, (d - 1) * CAPACITY + first_slot, count),
+            dst_ref=block(inbound, (GROUPS - d) * CAPACITY + first_slot, count),
+            send_sem=os.at[d, h], recv_sem=orr.at[d, h],
             device_id={"aux": aux, "occ": lax.rem(occ + d, GROUPS)}, device_id_type=MESH,
         )
 
@@ -227,10 +233,11 @@
     def arrived(kind, t, h):
         z_copy(kind, t, h).wait_recv()
 
-    def pass_on(kind, t, then):
+    def pass_on(kind, *pairs):
         for h in range(PARTS):
-            arrived(kind, t, h)
-            send(kind, then, h)
+            for t, then in pairs:
+                arrived(kind, t, h)
+                send(kind, then, h)
 
     def first_product(n):
         zo = owner_z(n)
@@ -378,7 +385,8 @@
             def _(s):
                 pool[(d - 1) * CAPACITY + s] = mine[table_s[d, s]]
 
-            occ_copy(d).start()
+            for h in range(2):
+                occ_copy(d, h).start()
 
         @pl.loop(0, CAPACITY)
         def _(s):
@@ -396,8 +404,8 @@
         for n in (4, 5):
             partial_products(kind, n)
         between(2)
-        for j in range(2):
-            for h in range(PARTS):
+        for h in range(PARTS):
+            for j in range(2):
                 arrived(kind, 2 + j, h)
                 accumulate(kind, 2 + j, j, h)
                 send(kind, 4 + j, h)
@@ -416,24 +424,22 @@
             send(kind, 7, h)
             send(kind, 8, h)
 
-    @pl.loop(0, 2)
-    def _(j):
-        @pl.loop(0, 2)
-        def _(i):
-            first_product(2 * i + j)
-
-        for n in range(2):
-
-            @pl.when(j == n)
-            def _():
-                start(end_copies(OWN, n))
-
-        start(x_copies(OWN, 2 + j))
+    first_product(0)
+    first_product(2)
+    pl.semaphore_wait(barrier, len(near) + GROUPS - 1)
+    start(end_copies(OWN, 0))
+    start(x_copies(OWN, 2))
+    first_product(1)
+    start(end_copies(OWN, 1))
+    first_product(3)
+    start(x_copies(OWN, 3))
 
     @pl.loop(4, NZ)
     def _(n):
         first_product(n)
 
+    to_table.wait()
+    to_place.wait()
     begin_occ()
 
     def rest(k):
@@ -443,41 +449,39 @@
 
     inward(OWN, rest)
 
-    pass_on(OWN, 7, 9)
-    pass_on(OWN, 8, 10)
-
     for n in range(2):
         end_sent(OWN, n)
 
     @pl.loop(2, NZ)
     def _(n):
         x_sent(OWN, n)
-
-    for d in range(1, GROUPS):
-        occ_copy(d).wait_recv()
-        occ_copy(d).wait_send()
 
     def take_partners(n):
         zo = owner_z(n)
         for k in range(NX):
             mine[zo * NX + k] = inbound[place_s[0, occ * GO + zo * NX + k]]
 
-    for n in range(2):
-        take_partners(n)
-        start(end_copies(PAR, n))
-        take_partners(n + 2)
-        start(x_copies(PAR, n + 2))
-
-    pass_on(OWN, 9, 11)
+    pass_on(OWN, (7, 9), (8, 10))
+    for d in range(1, GROUPS):
+        for h in range(2):
+            occ_copy(d, h).wait_recv()
+            occ_copy(d, h).wait_send()
+    take_partners(0)
+    start(end_copies(PAR, 0))
+    take_partners(2)
+    start(x_copies(PAR, 2))
+    take_partners(1)
+    start(end_copies(PAR, 1))
+    take_partners(3)
+    start(x_copies(PAR, 3))
+    pass_on(OWN, (9, 11))
 
     @pl.loop(4, NZ)
     def _(n):
         take_partners(n)
+        start(x_copies(PAR, n))
 
     def between(k):
-        if k < 2:
-            start(x_copies(PAR, 4 + k))
-            start(x_copies(PAR, 6 + k))
         if k == 0:
             density(OWN, 5)
         if k == 2:
@@ -495,11 +499,10 @@
 
     inward(PAR, between)
 
-    pass_on(PAR, 7, 9)
-    pass_on(PAR, 8, 10)
+    pass_on(PAR, (7, 9), (8, 10))
     density(PAR, 5)
     start(x_copies(OUT, 7))
-    pass_on(PAR, 9, 11)
+    pass_on(PAR, (9, 11))
     density(PAR, 4)
     start(x_copies(OUT, 6))
     density(PAR, 3)
@@ -577,8 +580,8 @@
             pltpu.SMEM((8, total), jnp.int32),
             dma((3, NZ, NX)),
             dma((3, NZ, NX)),
-            dma((GROUPS,)),
-            dma((GROUPS,)),
+            dma((GROUPS, 2)),
+            dma((GROUPS, 2)),
             dma((2, 12, PARTS)),
             dma((2, 12, PARTS)),
             dma((size // SUB + 1, atoms // PANEL)),

time: 270 us -> 268 us (level)
  Pallas kernels: 260 us -> 257 us
    pallas_call x1, Pallas kernels: 260 us -> 257 us  [local(): pl.pallas_call(kernel, out_shape=jax.ShapeDtypeStruct((size, slices, widt...]
where the time goes in v4:
time: 268 us; the launch traced here: 265 us
  Pallas kernels  257 us (96%)
  local copies, waits for them, and re-layouts  8.1 us (3%)
    pallas_call x1, Pallas kernels, local(): pl.pallas_call(kernel, out_shape=jax.ShapeDtypeStruct((size, slices, widt...  257 us
    transpose x1, local copies, waits for them, and re-layouts, local(): return jnp.transpose(out, (1, 0, 2))  6.63 us

profile of v4, /device:TPU:2, one launch (start us, length us, event | category | flops | bytes accessed | tf_op | source)
XLA Modules:
  0.0 265.5 jit_solution(6452460088973809038)
XLA Ops:
  0.0 1.5 copy.6.partner_col_ref
  1.5 257.3 %shard_map.55 = f32[32,64,512]{2,1,0:T(8,128)} custom-call(s32[256]{0:T(256)} %bitcast.5, f32[256]{0:T(256)} %occupied_ref.1, s32[1,256]{1,0:T(1,128)} %bitcast.6, s32[256,1]{1,0:T(8,128)} %copy.6.partner_col_ref, f32[64,32,768]{2,1,0:T(8,128)} %half_ref.1, f32[768,512]{1,0:T(8,128)} %orbitals_ref.1, f32[1,512]{1,0:T(1,128)} %bitcast.7), custom_call_target="tpu_custom_call" | custom-call | tf_op jit(solution)/shard_map/pallas_call | solution.py:549
  258.8 6.6 %copy.7 = f32[64,32,512]{2,1,0:T(8,128)} copy(f32[64,32,512]{2,0,1:T(8,128)} %bitcast.4) | data formatting | bytes 8388608 | tf_op jit(solution)/shard_map/transpose | solution.py:601
